TPU v7x, 32 devices: a whole 2x2x4 slice. The times are simulated.
32 devices in a mesh: rack: 4 (over z), dev: 8 (over y, x, core).
Axes of the slice: x: 2, y: 2, z: 4, core: 2. Of those that a mesh axis runs over, the one named last changes fastest.
Arguments:
- span_store: bfloat16 [704, 64, 1024], P(('rack', 'dev')), may hold values from -6 to 6
- helper_offset: int32 [22], replicated, may hold values from 1 to 31, as said below
- plane_index: int32 [64, 16], replicated, may hold values from 0 to 63, as said below
- coupling_pair: int32 [64, 11, 16], P(('rack', 'dev')), may hold values from 0 to 10
- decode_matrix: float32 [64, 4, 11], P(('rack', 'dev')), may hold values from -1.75 to 1.75
- recouple_pair: int32 [64, 64], P(('rack', 'dev')), may hold values from 0 to 63
Outputs:
- rebuilt: bfloat16 [64, 64, 1024], P(('rack', 'dev'))
Inputs may be any that keep to these rules, and one draw needn't show every extreme that they name: 22 distinct values; helper slot j of a stripe of device p is always slot j of device p + helper_offset[j] (mod the device count). `plane_index`: each row lists in increasing order the 16 indices z whose base-4 digit number y equals x, for the stripe's lost node (x, y), x below 4 and y below 3.
All inputs are finite; a program needn't handle non-finite values.
Results may differ from a plain program's by a relative error of at most 0.001.
Values may be sent and summed in bfloat16 or wider, within the bound.
No kernel may reach another device: no remote copies, remote signals or barrier semaphores. Data moves between devices by JAX's collectives and lax.ppermute only.
A program may use at most 64 MiB of HBM per device.

v0:
```python
import functools

import jax
import jax.numpy as jnp
from jax import lax
from jax.experimental import pallas as pl
from jax.experimental.pallas import tpu as pltpu
from jax.sharding import PartitionSpec as P

AXES = ("rack", "dev")
COUPLING = 0.6
HIGHEST = lax.Precision.HIGHEST
TOGETHER = 8
HBM = pl.BlockSpec(memory_space=pltpu.HBM)
VMEM = pl.BlockSpec(memory_space=pltpu.VMEM)


def near_masks(rack_count):
    return list(range(rack_count - 2, 0, -1))


def far_peer(me, index, rack_count, dev_count):
    if rack_count == 1:
        return index
    rack = me // dev_count
    first = jnp.minimum(rack, (rack_count - 1) - rack)
    rank = first if index % 2 == 0 else (rack_count - 1) - first
    return rank * dev_count + index // 2


def far_rules(rack_count, dev_count):
    size = dev_count * (2 if rack_count > 1 else 1)
    return [functools.partial(lambda i, me: far_peer(me, i, rack_count, dev_count), i) for i in range(size)]


def near_rules(mask, dev_count):
    return [functools.partial(lambda m, me: me ^ m, mask * dev_count + d) for d in range(dev_count)]


def pick_kernel(layout, in_hbm, helpers, offset_hbm, planes_hbm, store_ref, *refs):
    outs = refs[: len(layout)]
    held, staged, offset, planes, table, load_sem, store_sem, small_sem = refs[len(layout) :]
    slots, sub_total, _ = store_ref.shape
    plane_count = planes.shape[0]
    device_count = table.shape[0]
    small = [
        pltpu.make_async_copy(offset_hbm, offset, small_sem.at[0]),
        pltpu.make_async_copy(planes_hbm, planes, small_sem.at[1]),
    ]
    for copy in small:
        copy.start()
    me = lax.axis_index("rack") * lax.axis_size("dev") + lax.axis_index("dev")
    row = lax.broadcasted_iota(jnp.int32, (plane_count, sub_total), 0)
    col = lax.broadcasted_iota(jnp.int32, (plane_count, sub_total), 1)
    coarse, fine = row // 4, row % 4
    for i in range(device_count):
        table[i] = -1
    small[0].wait()
    for j in range(slots):
        table[offset[j]] = j
    order = sorted(range(len(layout)), key=lambda o: o not in in_hbm)
    blocks = [(o, k, rule) for o in order for k, rule in enumerate(layout[o])]
    wanted = []
    for b, (_, _, rule) in enumerate(blocks):
        peer = rule(me)
        gap = me - peer
        found = table[jnp.where(gap < 0, gap + device_count, gap)]
        slot = jnp.maximum(found, 0)
        copy = pltpu.make_async_copy(store_ref.at[slot], held.at[b], load_sem.at[b])
        wanted.append((found >= 0, peer * (slots // helpers) + slot // helpers, copy))

        @pl.when(found >= 0)
        def _():
            copy.start()

    small[1].wait()
    stores = []
    for first in range(0, len(blocks), TOGETHER):
        some = range(first, min(first + TOGETHER, len(blocks)))
        for b in some:
            used, _, copy = wanted[b]

            @pl.when(used)
            def _():
                copy.wait()

        for b in some:
            used, stripe, _ = wanted[b]
            o, k, _ = blocks[b]
            start, step, jump = planes[0, stripe], planes[1, stripe], planes[4, stripe]
            picked = (col == start + (jump - start) * coarse + (step - start) * fine).astype(jnp.float32)
            rows = jnp.dot(picked.astype(held.dtype), held[b], preferred_element_type=jnp.float32)
            rows = jnp.where(used, rows, 0.0).astype(held.dtype)
            into = staged if o in in_hbm else outs[o]
            into[pl.ds(k * plane_count, plane_count)] = rows
        done = [b for b in some if blocks[b][0] in in_hbm]
        if done:
            part = pl.ds(done[0] * plane_count, len(done) * plane_count)
            stores.append(pltpu.make_async_copy(staged.at[part], outs[order[0]].at[part], store_sem.at[len(stores)]))
            stores[-1].start()
    for copy in stores:
        copy.wait()


def pick_rows(layout, in_hbm, helpers, device_count, helper_offset, planes, store):
    _, sub_total, columns = store.shape
    plane_count = planes.shape[0]
    total = sum(len(rules) for rules in layout)
    direct = max([len(layout[o]) for o in in_hbm], default=1)
    return pl.pallas_call(
        functools.partial(pick_kernel, layout, in_hbm, helpers),
        out_shape=[jax.ShapeDtypeStruct((len(rules) * plane_count, columns), store.dtype) for rules in layout],
        in_specs=[HBM] * 3,
        out_specs=[HBM if o in in_hbm else VMEM for o in range(len(layout))],
        scratch_shapes=[
            pltpu.VMEM((total, sub_total, columns), store.dtype),
            pltpu.VMEM((direct * plane_count, columns), store.dtype),
            pltpu.SMEM(helper_offset.shape, jnp.int32),
            pltpu.SMEM(planes.shape, jnp.int32),
            pltpu.SMEM((device_count,), jnp.int32),
            pltpu.SemaphoreType.DMA((total,)),
            pltpu.SemaphoreType.DMA((pl.cdiv(direct, TOGETHER),)),
            pltpu.SemaphoreType.DMA((2,)),
        ],
        cost_estimate=pl.CostEstimate(
            flops=2 * total * plane_count * sub_total * columns,
            bytes_accessed=2 * total * (sub_total + plane_count) * columns,
            transcendentals=0,
        ),
        compiler_params=pltpu.CompilerParams(
            vmem_limit_bytes=2 * total * (sub_total + 3 * plane_count) * columns + (4 << 20)
        ),
        name="pick_rows",
    )(*(pltpu.with_memory_space_constraint(x, pltpu.HBM) for x in (helper_offset, planes, store)))


def rebuild_kernel(counts, matrix_ref, *refs):
    rows_refs, (out_ref, *scratch) = refs[: len(counts)], refs[len(counts) :]
    out_rows = out_ref.shape[0]
    rows = rows_refs[0]
    if len(counts) > 1:
        rows, at = scratch[0], 0
        for r, count in zip(rows_refs, counts):
            rows[pl.ds(at, count)] = r[pl.ds(0, count)]
            at += count
    three = jnp.dot(matrix_ref[...], rows[...], preferred_element_type=jnp.float32)
    total = three[2 * out_rows :] + three[out_rows : 2 * out_rows] + three[:out_rows]
    out_ref[...] = total.astype(out_ref.dtype)


def rebuild(matrix, pieces, counts):
    out_rows = matrix.shape[0] // 3
    columns = pieces[0].shape[1]
    total = sum(counts)
    return pl.pallas_call(
        functools.partial(rebuild_kernel, counts),
        out_shape=jax.ShapeDtypeStruct((out_rows, columns), jnp.bfloat16),
        in_specs=[VMEM] * (1 + len(pieces)),
        out_specs=VMEM,
        scratch_shapes=[pltpu.VMEM((total, columns), jnp.bfloat16)] if len(pieces) > 1 else [],
        cost_estimate=pl.CostEstimate(
            flops=6 * out_rows * total * columns, bytes_accessed=2 * columns * (total + out_rows), transcendentals=0
        ),
        compiler_params=pltpu.CompilerParams(vmem_limit_bytes=(4 * total + 16 * out_rows) * columns + (4 << 20)),
        name="rebuild",
    )(matrix, *pieces)


def three_terms(x):
    terms = []
    for _ in range(3):
        terms.append(lax.reduce_precision(x, 8, 7))
        x = x - terms[-1]
    return jnp.concatenate(terms, 0).astype(jnp.bfloat16)


def repair_matrix(decode_block, pair_block, recouple_pairs, sources, peers):
    stripes_here, helpers, plane_count = pair_block.shape
    group_size = decode_block.shape[1]
    helper_ids = jnp.arange(helpers, dtype=jnp.int32)
    choose = (pair_block[..., None] == helper_ids).astype(jnp.float32)
    coupled = (pair_block != helper_ids[None, :, None]).astype(jnp.float32)
    unmix = (jnp.eye(helpers, dtype=jnp.float32)[None, :, None, :] - COUPLING * coupled[..., None] * choose) / (
        1.0 - COUPLING * COUPLING
    )
    sectioned = jnp.einsum("sth,shzg->sztg", decode_block, unmix, precision=HIGHEST)
    sub_count = plane_count * group_size
    rows_in = jnp.arange(peers.shape[0] * plane_count, dtype=jnp.int32)
    peer_of_row = jnp.repeat(peers, plane_count)
    at_row = (sources.reshape(stripes_here, helpers)[..., None] == peer_of_row).astype(jnp.float32)
    spread = jnp.einsum(
        "sag,sgr->sar", sectioned.reshape(stripes_here, sub_count, helpers), at_row, precision=HIGHEST
    )
    same_plane = jnp.arange(sub_count, dtype=jnp.int32)[:, None] // group_size == rows_in[None, :] % plane_count
    spread = jnp.where(same_plane[None], spread, 0.0)
    sub_ids = jnp.arange(sub_count, dtype=jnp.int32)
    pick = (recouple_pairs[..., None] == sub_ids).astype(jnp.float32)
    distinct = (recouple_pairs != sub_ids[None, :]).astype(jnp.float32)
    mixing = jnp.eye(sub_count, dtype=jnp.float32)[None] + COUPLING * distinct[..., None] * pick
    whole = jnp.einsum("sab,sbc->sac", mixing, spread, precision=HIGHEST)
    return whole.reshape(stripes_here * sub_count, peers.shape[0] * plane_count)


def swap(x, mask, device_count):
    return lax.ppermute(x, AXES, [(q, q ^ mask) for q in range(device_count)])


def body(span_store, helper_offset, plane_index, coupling_pair, decode_matrix, recouple_pair):
    rack_count, dev_count = lax.axis_size("rack"), lax.axis_size("dev")
    device_count = rack_count * dev_count
    me = lax.axis_index("rack") * dev_count + lax.axis_index("dev")
    columns = span_store.shape[-1]
    stripes_here, helpers, plane_count = coupling_pair.shape
    sub_count = recouple_pair.shape[1]
    near = near_masks(rack_count)
    pick = functools.partial(
        pick_rows, helpers=helpers, device_count=device_count, helper_offset=helper_offset, planes=plane_index.T, store=span_store
    )
    early = near[:2]
    outgoing = []
    if early:
        outgoing += pick([near_rules(m, dev_count) for m in early], ())
    layout = [near_rules(m, dev_count) for m in near[len(early):]] + [far_rules(rack_count, dev_count)]
    outgoing += pick(layout, (len(layout) - 1,))
    across = [swap(x, m * dev_count, device_count) for m, x in zip(near, outgoing)]
    groups = None
    if rack_count > 1:
        groups = [
            [rack * dev_count + d for d in range(dev_count) for rack in (r, rack_count - 1 - r)]
            for r in range(rack_count // 2)
        ]
    blocks = outgoing[-1].reshape(-1, plane_count, columns)
    far = lax.all_to_all(blocks, AXES, 0, 0, axis_index_groups=groups, tiled=True).reshape(-1, columns)
    peers = [far_peer(me, i, rack_count, dev_count) for i in range(far.shape[0] // plane_count)]
    arrived, counts = [far], [far.shape[0]]
    if near:
        chips = range(dev_count // 2)
        blocks = [x.reshape(-1, 2, plane_count, columns) for x in across]
        crossed = swap(jnp.concatenate([x[chip, 1] for chip in chips for x in blocks], 0), 1, device_count)
        both = len(near) * plane_count
        arrived += across + [crossed]
        counts += [plane_count] * len(near) + [both]
        peers += [me ^ (m * dev_count) for m in near] + [me ^ (m * dev_count) ^ 1 for m in near]
        for chip in chips[1:]:
            part = [x[chip, 0] for x in blocks] + [crossed[both * chip : both * (chip + 1)]]
            arrived.append(swap(jnp.concatenate(part, 0), 2 * chip, device_count))
            counts.append(2 * both)
            peers += [me ^ (m * dev_count + 2 * chip + core) for core in (0, 1) for m in near]
    sources = (me + helper_offset) % device_count
    peers = jnp.stack([jnp.asarray(p, jnp.int32) for p in peers])
    whole = three_terms(repair_matrix(decode_matrix, coupling_pair, recouple_pair, sources, peers))
    return rebuild(whole, arrived, counts).reshape(stripes_here, sub_count, columns)


def solution(mesh):
    split = ("rack", "dev")
    placed = (
        P(split, None, None),
        P(),
        P(),
        P(split, None, None),
        P(split, None, None),
        P(split, None),
    )
    return jax.shard_map(body, mesh=mesh, in_specs=placed, out_specs=P(split, None, None), check_vma=False)
```

profile of v0, /device:TPU:0, one launch (start us, length us, event | category | flops | bytes accessed | tf_op | source)
XLA Modules:
  0.0 49.1 jit_solution(11708761704004619441)
XLA Ops:
  0.0 3.3 %pick_rows.2 = bf16[256,1024]{1,0:T(8,128)(2,1)} custom-call(s32[22]{0:T(128)} %offset_hbm.3, s32[16,64]{1,0:T(8,128)} %bitcast.111, bf16[22,64,1024]{2,1,0:T(8,128)(2,1)} %store_ref.3), custom_call_target="tpu_custom_call" | custom-call | flops 33554432 | bytes 2621440 | tf_op jit(solution)/shard_map/pick_rows/pallas_call | solution.py:110
  3.4 8.4 %all-to-all-start = ((bf16[16,16,1024]{2,1,0:T(8,128)(2,1)}), bf16[16,16,1024]{2,1,0:T(8,128)(2,1)S(1)}, u32[]{:S(2)}, u32[]{:S(2)}) async-start(bf16[16,16,1024]{2,1,0:T(8,128)(2,1)} %bitcast.38), calls=%async_computation | async-start | bytes 1048576 | tf_op jit(solution)/shard_map/all_to_all | solution.py:233
  11.7 2.6 %pick_rows.3 = (bf16[128,1024]{1,0:T(8,128)(2,1)S(1)}, bf16[128,1024]{1,0:T(8,128)(2,1)S(1)}) custom-call(s32[22]{0:T(128)} %offset_hbm.3, s32[16,64]{1,0:T(8,128)} %bitcast.112, bf16[22,64,1024]{2,1,0:T(8,128)(2,1)} %store_ref.3), custom_call_target="tpu_custom_call" | custom-call | flops 33554432 | bytes 2621440 | tf_op jit(solution)/shard_map/pick_rows/pallas_call | solution.py:110
  14.4 1.1 %collective-permute-start = (bf16[128,1024]{1,0:T(8,128)(2,1)S(1)}, bf16[128,1024]{1,0:T(8,128)(2,1)S(1)}, u32[]{:S(2)}, u32[]{:S(2)}) collective-permute-start(bf16[128,1024]{1,0:T(8,128)(2,1)S(1)} %get-tuple-element.7), channel_id=1, source_target_pairs={{0,16},{1,17},{2,18},{3,19},{4,20},{5,21},{6,22},{7,23},{8,24},{9,... | collective-permute-start | bytes 786440 | tf_op jit(solution)/shard_map/ppermute | solution.py:205
  15.5 3.2 %collective-permute-start.1 = (bf16[128,1024]{1,0:T(8,128)(2,1)S(1)}, bf16[128,1024]{1,0:T(8,128)(2,1)S(1)}, u32[]{:S(2)}, u32[]{:S(2)}) collective-permute-start(bf16[128,1024]{1,0:T(8,128)(2,1)S(1)} %get-tuple-element.8), channel_id=1, source_target_pairs={{0,8},{1,9},{2,10},{3,11},{4,12},{5,13},{6,14},{7,15},{8,0},{9,1},... | collective-permute-start | bytes 786440 | tf_op jit(solution)/shard_map/ppermute | solution.py:205
  18.8 0.1 eq.89
  18.9 0.1 stack.131
  19.0 0.1 broadcast_in_dim.11
  19.1 0.1 eq.91
  19.2 0.3 convolution_bitcast_fusion
  19.5 0.1 copy.11
  19.6 0.1 broadcast_compare_fusion
  19.7 0.3 convolution_select_fusion
  20.1 0.4 fusion.10
  20.5 15.9 %collective-permute-done.refs_1_ = bf16[128,1024]{1,0:T(8,128)(2,1)S(1)} collective-permute-done((bf16[128,1024]{1,0:T(8,128)(2,1)S(1)}, bf16[128,1024]{1,0:T(8,128)(2,1)S(1)}, u32[]{:S(2)}, u32[]{:S(2)}) %collective-permute-start) | collective-permute-done | bytes 262176 | tf_op jit(solution)/shard_map/ppermute | solution.py:205
  36.5 0.1 collective-permute-start.2
  36.6 1.5 %collective-permute-done.2.refs_3_ = bf16[128,1024]{1,0:T(8,128)(2,1)S(1)} collective-permute-done((bf16[128,1024]{1,0:T(8,128)(2,1)S(1)}, bf16[128,1024]{1,0:T(8,128)(2,1)S(1)}, u32[]{:S(2)}, u32[]{:S(2)}) %collective-permute-start.2) | collective-permute-done | bytes 262176 | tf_op jit(solution)/shard_map/ppermute | solution.py:205
  38.1 1.5 %collective-permute-start.3 = (bf16[64,1024]{1,0:T(8,128)(2,1)S(1)}, bf16[64,1024]{1,0:T(8,128)(2,1)S(1)}, u32[]{:S(2)}, u32[]{:S(2)}) collective-permute-start(bf16[64,1024]{1,0:T(8,128)(2,1)S(1)} %pad_maximum_fusion.1), channel_id=1, source_target_pairs={{0,2},{1,3},{2,0},{3,1},{4,6},{5,7},{6,4},{7,5},{8,10},{9,11},{10,... | collective-permute-start | bytes 393224 | tf_op jit(solution)/shard_map/ppermute | solution.py:205
  39.7 1.5 %collective-permute-start.4 = (bf16[64,1024]{1,0:T(8,128)(2,1)S(1)}, bf16[64,1024]{1,0:T(8,128)(2,1)S(1)}, u32[]{:S(2)}, u32[]{:S(2)}) collective-permute-start(bf16[64,1024]{1,0:T(8,128)(2,1)S(1)} %pad_maximum_fusion.2), channel_id=1, source_target_pairs={{0,4},{1,5},{2,6},{3,7},{4,0},{5,1},{6,2},{7,3},{8,12},{9,13},{10,... | collective-permute-start | bytes 393224 | tf_op jit(solution)/shard_map/ppermute | solution.py:205
  41.2 0.6 %collective-permute-start.5 = (bf16[64,1024]{1,0:T(8,128)(2,1)S(1)}, bf16[64,1024]{1,0:T(8,128)(2,1)S(1)}, u32[]{:S(2)}, u32[]{:S(2)}) collective-permute-start(bf16[64,1024]{1,0:T(8,128)(2,1)S(1)} %pad_maximum_fusion.3), channel_id=1, source_target_pairs={{0,6},{1,7},{2,4},{3,5},{4,2},{5,3},{6,0},{7,1},{8,14},{9,15},{10,... | collective-permute-start | bytes 393224 | tf_op jit(solution)/shard_map/ppermute | solution.py:205
  41.8 0.1 reduce-precision_convert_fusion.1
  41.9 2.1 %collective-permute-done.3.refs_4_ = bf16[64,1024]{1,0:T(8,128)(2,1)S(1)} collective-permute-done((bf16[64,1024]{1,0:T(8,128)(2,1)S(1)}, bf16[64,1024]{1,0:T(8,128)(2,1)S(1)}, u32[]{:S(2)}, u32[]{:S(2)}) %collective-permute-start.3) | collective-permute-done | bytes 131104 | tf_op jit(solution)/shard_map/ppermute | solution.py:205
  44.0 3.8 %collective-permute-done.4.refs_5_ = bf16[64,1024]{1,0:T(8,128)(2,1)S(1)} collective-permute-done((bf16[64,1024]{1,0:T(8,128)(2,1)S(1)}, bf16[64,1024]{1,0:T(8,128)(2,1)S(1)}, u32[]{:S(2)}, u32[]{:S(2)}) %collective-permute-start.4) | collective-permute-done | bytes 131104 | tf_op jit(solution)/shard_map/ppermute | solution.py:205
  47.8 1.3 %rebuild.1 = bf16[128,1024]{1,0:T(8,128)(2,1)} custom-call(bf16[384,512]{1,0:T(8,128)(2,1)S(1)} %pad_maximum_fusion.matrix_ref, bf16[256,1024]{1,0:T(8,128)(2,1)S(1)} %bitcast.99, bf16[128,1024]{1,0:T(8,128)(2,1)S(1)} %collective-permute-done.refs_1_, bf16[128,1024]{1,0:T(8,128)(2,1)S(1)} %collective-permute-done.1.refs_2_, ...), custom_call_target="tpu_custom_call" | custom-call | flops 402653184 | bytes 1310720 | tf_op jit(solution)/shard_map/rebuild/pallas_call | solution.py:155
  (35 shorter events, 0.2 us)
Async XLA Ops:
  0.0 19.2 %copy-start = (f32[2,4,11]{2,1,0:T(4,128)S(1)}, f32[2,4,11]{2,1,0:T(4,128)}, u32[]{:S(2)}) copy-start(f32[2,4,11]{2,1,0:T(4,128)} %param.10) | copy-start | bytes 1060
  0.0 18.7 %copy-start.3 = (s32[22]{0:T(128)S(1)}, s32[22]{0:T(128)}, u32[]{:S(2)}) copy-start(s32[22]{0:T(128)} %offset_hbm.3) | copy-start | bytes 268
  0.0 18.8 %copy-start.1 = (s32[2,11,16]{2,0,1:T(2,128)S(1)}, s32[2,11,16]{2,0,1:T(2,128)}, u32[]{:S(2)}) copy-start(s32[2,11,16]{2,0,1:T(2,128)} %param.9) | copy-start | bytes 4228
  3.3 15.6 %copy-start.2 = (s32[2,64]{1,0:T(2,128)S(1)}, s32[2,64]{1,0:T(2,128)}, u32[]{:S(2)}) copy-start(s32[2,64]{1,0:T(2,128)} %param.11) | copy-start | bytes 1540
  3.4 44.5 %all-to-all-start = ((bf16[16,16,1024]{2,1,0:T(8,128)(2,1)}), bf16[16,16,1024]{2,1,0:T(8,128)(2,1)S(1)}, u32[]{:S(2)}, u32[]{:S(2)}) async-start(bf16[16,16,1024]{2,1,0:T(8,128)(2,1)} %bitcast.38), calls=%async_computation | async-start | bytes 1048576 | tf_op jit(solution)/shard_map/all_to_all | solution.py:233
  14.4 22.0 %collective-permute-start = (bf16[128,1024]{1,0:T(8,128)(2,1)S(1)}, bf16[128,1024]{1,0:T(8,128)(2,1)S(1)}, u32[]{:S(2)}, u32[]{:S(2)}) collective-permute-start(bf16[128,1024]{1,0:T(8,128)(2,1)S(1)} %get-tuple-element.7), channel_id=1, source_target_pairs={{0,16},{1,17},{2,18},{3,19},{4,20},{5,21},{6,22},{7,23},{8,24},{9,... | collective-permute-start | bytes 786440 | tf_op jit(solution)/shard_map/ppermute | solution.py:205
  15.5 20.9 %collective-permute-start.1 = (bf16[128,1024]{1,0:T(8,128)(2,1)S(1)}, bf16[128,1024]{1,0:T(8,128)(2,1)S(1)}, u32[]{:S(2)}, u32[]{:S(2)}) collective-permute-start(bf16[128,1024]{1,0:T(8,128)(2,1)S(1)} %get-tuple-element.8), channel_id=1, source_target_pairs={{0,8},{1,9},{2,10},{3,11},{4,12},{5,13},{6,14},{7,15},{8,0},{9,1},... | collective-permute-start | bytes 786440 | tf_op jit(solution)/shard_map/ppermute | solution.py:205
  36.5 1.6 %collective-permute-start.2 = (bf16[128,1024]{1,0:T(8,128)(2,1)S(1)}, bf16[128,1024]{1,0:T(8,128)(2,1)S(1)}, u32[]{:S(2)}, u32[]{:S(2)}) collective-permute-start(bf16[128,1024]{1,0:T(8,128)(2,1)S(1)} %fusion.14), channel_id=1, source_target_pairs={{0,1},{1,0},{2,3},{3,2},{4,5},{5,4},{6,7},{7,6},{8,9},{9,8},{10,11... | collective-permute-start | bytes 786440 | tf_op jit(solution)/shard_map/ppermute | solution.py:205
  38.1 5.9 %collective-permute-start.3 = (bf16[64,1024]{1,0:T(8,128)(2,1)S(1)}, bf16[64,1024]{1,0:T(8,128)(2,1)S(1)}, u32[]{:S(2)}, u32[]{:S(2)}) collective-permute-start(bf16[64,1024]{1,0:T(8,128)(2,1)S(1)} %pad_maximum_fusion.1), channel_id=1, source_target_pairs={{0,2},{1,3},{2,0},{3,1},{4,6},{5,7},{6,4},{7,5},{8,10},{9,11},{10,... | collective-permute-start | bytes 393224 | tf_op jit(solution)/shard_map/ppermute | solution.py:205
  39.7 8.1 %collective-permute-start.4 = (bf16[64,1024]{1,0:T(8,128)(2,1)S(1)}, bf16[64,1024]{1,0:T(8,128)(2,1)S(1)}, u32[]{:S(2)}, u32[]{:S(2)}) collective-permute-start(bf16[64,1024]{1,0:T(8,128)(2,1)S(1)} %pad_maximum_fusion.2), channel_id=1, source_target_pairs={{0,4},{1,5},{2,6},{3,7},{4,0},{5,1},{6,2},{7,3},{8,12},{9,13},{10,... | collective-permute-start | bytes 393224 | tf_op jit(solution)/shard_map/ppermute | solution.py:205
  41.2 6.6 %collective-permute-start.5 = (bf16[64,1024]{1,0:T(8,128)(2,1)S(1)}, bf16[64,1024]{1,0:T(8,128)(2,1)S(1)}, u32[]{:S(2)}, u32[]{:S(2)}) collective-permute-start(bf16[64,1024]{1,0:T(8,128)(2,1)S(1)} %pad_maximum_fusion.3), channel_id=1, source_target_pairs={{0,6},{1,7},{2,4},{3,5},{4,2},{5,3},{6,0},{7,1},{8,14},{9,15},{10,... | collective-permute-start | bytes 393224 | tf_op jit(solution)/shard_map/ppermute | solution.py:205
where the time goes:
time: 49.5 us; the launch traced here: 49.1 us
  waiting for transfers between devices  23.3 us (47%)
  starting transfers between devices  16.5 us (33%)
  Pallas kernels  7.24 us (15%)
  matrix products  1.06 us (2%)
  local copies, waits for them, and re-layouts  0.57 us (1%)
    ppermute x6, waiting for transfers between devices, swap(): return lax.ppermute(x, AXES, [(q, q ^ mask) for q in range(device_count)])  23.3 us
    all_to_all x1, starting transfers between devices, body(): lax.all_to_all(blocks, AXES, 0, 0, axis_index_groups=groups, tiled=True)  8.38 us
    ppermute x6, starting transfers between devices, swap(): return lax.ppermute(x, AXES, [(q, q ^ mask) for q in range(device_count)])  8.09 us
    pallas_call x2, Pallas kernels, pick_rows(): pl.pallas_call(functools.partial(pick_kernel, layout, in_hbm, helpers), o...  5.96 us
    pallas_call x1, Pallas kernels, rebuild(): pl.pallas_call(functools.partial(rebuild_kernel, counts), out_shape=jax.S...  1.28 us
  transfers between devices with their start and end apart: 7, of which 4 were waited for; matrix products, arithmetic and copies ran while one was open for 4% of the time, Pallas kernels for 5%

commit v1 on v0

v1 whole, which is shorter than its diff:
```python
import functools

import jax
import jax.numpy as jnp
from jax import lax
from jax.experimental import pallas as pl
from jax.experimental.pallas import tpu as pltpu
from jax.sharding import PartitionSpec as P

AXES = ("rack", "dev")
COUPLING = 0.6
HIGHEST = lax.Precision.HIGHEST
TOGETHER = 8
AHEAD = 2
TERMS = 3
PARTS = 2
HBM = pl.BlockSpec(memory_space=pltpu.HBM)
VMEM = pl.BlockSpec(memory_space=pltpu.VMEM)


def near_masks(rack_count):
    return list(range(rack_count - 2, 0, -1))


def far_peer(me, index, rack_count, dev_count):
    if rack_count == 1:
        return index
    rack = me // dev_count
    first = jnp.minimum(rack, (rack_count - 1) - rack)
    rank = first if index % 2 == 0 else (rack_count - 1) - first
    return rank * dev_count + index // 2


def ahead_chips(rack_count, dev_count):
    chips = dev_count // 2
    return list(range(chips - min(AHEAD, chips - 1), chips)) if near_masks(rack_count) else []


def outgoing_rules(near, ahead, rack_count, dev_count):
    def to(mask):
        return lambda me: me ^ mask

    counts = [dev_count - 2 * len(ahead)] + [dev_count] * (len(near) - 1) if near else []
    rules = [[to(m * dev_count + d) for d in range(count)] for m, count in zip(near, counts)]
    rules += [[to(near[0] * dev_count + 2 * chip + core) for core in (0, 1)] for chip in ahead]
    far_count = dev_count * (2 if rack_count > 1 else 1)
    rules.append([functools.partial(far_peer, index=i, rack_count=rack_count, dev_count=dev_count) for i in range(far_count)])
    return rules


def pick_kernel(rules, helpers, offset_hbm, planes_hbm, store_ref, *refs):
    outs, (held, picked, offset, planes, table, load_sem, small_sem) = refs[:-7], refs[-7:]
    slots, sub_total, _ = store_ref.shape
    plane_count = planes.shape[0]
    device_count = table.shape[0]
    small = [
        pltpu.make_async_copy(offset_hbm, offset, small_sem.at[0]),
        pltpu.make_async_copy(planes_hbm, planes, small_sem.at[1]),
    ]
    loads = [pltpu.make_async_copy(store_ref.at[j], held.at[j], load_sem.at[j]) for j in range(slots)]
    for copy in small + loads:
        copy.start()
    me = lax.axis_index("rack") * lax.axis_size("dev") + lax.axis_index("dev")
    row = lax.broadcasted_iota(jnp.int32, (plane_count, sub_total), 0)
    col = lax.broadcasted_iota(jnp.int32, (plane_count, sub_total), 1)
    coarse, fine = row // 4, row % 4
    for i in range(device_count):
        table[i] = -1
    for copy in small:
        copy.wait()
    wanted = []
    for j in range(slots):
        gap = me - offset[j]
        peer = jnp.where(gap < 0, gap + device_count, gap)
        table[peer] = j
        stripe = peer * (slots // helpers) + j // helpers
        start = planes[0, stripe]
        wanted.append((start, planes[1, stripe] - start, planes[4, stripe] - start))
    for first in range(0, slots, TOGETHER):
        some = range(first, min(first + TOGETHER, slots))
        for j in some:
            loads[j].wait()
        for j in some:
            start, step, jump = wanted[j]
            mask = (col == start + jump * coarse + step * fine).astype(jnp.float32)
            rows = jnp.dot(mask.astype(held.dtype), held[j], preferred_element_type=jnp.float32)
            picked[j] = rows.astype(held.dtype)
    for out, receivers in zip(outs, rules):
        for k, receiver in enumerate(receivers):
            slot = table[receiver(me)]
            rows = jnp.where(slot >= 0, picked[jnp.maximum(slot, 0)], jnp.zeros((), held.dtype))
            out[pl.ds(k * plane_count, plane_count)] = rows


def pick_rows(rules, helpers, device_count, helper_offset, planes, store):
    slots, sub_total, columns = store.shape
    plane_count = planes.shape[0]
    counts = [len(r) * plane_count for r in rules]
    return pl.pallas_call(
        functools.partial(pick_kernel, rules, helpers),
        out_shape=[jax.ShapeDtypeStruct((count, columns), store.dtype) for count in counts],
        in_specs=[HBM] * 3,
        out_specs=[VMEM] * len(counts),
        scratch_shapes=[
            pltpu.VMEM((slots, sub_total, columns), store.dtype),
            pltpu.VMEM((slots, plane_count, columns), store.dtype),
            pltpu.SMEM(helper_offset.shape, jnp.int32),
            pltpu.SMEM(planes.shape, jnp.int32),
            pltpu.SMEM((device_count,), jnp.int32),
            pltpu.SemaphoreType.DMA((slots,)),
            pltpu.SemaphoreType.DMA((2,)),
        ],
        cost_estimate=pl.CostEstimate(
            flops=2 * slots * plane_count * sub_total * columns,
            bytes_accessed=2 * (slots * sub_total + sum(counts)) * columns,
            transcendentals=0,
        ),
        compiler_params=pltpu.CompilerParams(
            vmem_limit_bytes=2 * (slots * (sub_total + plane_count) + 2 * sum(counts)) * columns + (4 << 20)
        ),
        name="pick_rows",
    )(*(pltpu.with_memory_space_constraint(x, pltpu.HBM) for x in (helper_offset, planes, store)))


def put_kernel(rows_ref, out_ref, sem):
    copy = pltpu.make_async_copy(rows_ref, out_ref, sem)
    copy.start()
    copy.wait()


def put_in_hbm(rows):
    return pl.pallas_call(
        put_kernel,
        out_shape=jax.ShapeDtypeStruct(rows.shape, rows.dtype),
        in_specs=[VMEM],
        out_specs=HBM,
        scratch_shapes=[pltpu.SemaphoreType.DMA],
        cost_estimate=pl.CostEstimate(flops=0, bytes_accessed=4 * rows.size, transcendentals=0),
        compiler_params=pltpu.CompilerParams(vmem_limit_bytes=2 * rows.size + (4 << 20)),
        name="put_in_hbm",
    )(rows)


def rebuild_kernel(counts, matrix_ref, *refs):
    rows_refs, (out_ref, made, store_sem, *scratch) = refs[: len(counts)], refs[len(counts) :]
    out_rows = out_ref.shape[0]
    rows = rows_refs[0]
    if len(counts) > 1:
        rows, at = scratch[0], 0
        for r, count in zip(rows_refs, counts):
            rows[pl.ds(at, count)] = r[pl.ds(0, count)]
            at += count
    wide = out_ref.shape[1] // PARTS
    stores = []
    for c in range(PARTS):
        part = pl.ds(c * wide, wide)
        terms = jnp.dot(matrix_ref[...], rows[:, part], preferred_element_type=jnp.float32)
        total = terms[:out_rows]
        for t in range(1, TERMS):
            total += terms[t * out_rows : (t + 1) * out_rows]
        made[:, part] = total.astype(made.dtype)
        stores.append(pltpu.make_async_copy(made.at[:, part], out_ref.at[:, part], store_sem.at[c]))
        stores[-1].start()
    for copy in stores:
        copy.wait()


def rebuild(matrix, pieces, counts):
    out_rows = matrix.shape[0] // TERMS
    columns = pieces[0].shape[1]
    total = sum(counts)
    return pl.pallas_call(
        functools.partial(rebuild_kernel, counts),
        out_shape=jax.ShapeDtypeStruct((out_rows, columns), jnp.bfloat16),
        in_specs=[VMEM] * (1 + len(pieces)),
        out_specs=HBM,
        scratch_shapes=[pltpu.VMEM((out_rows, columns), jnp.bfloat16), pltpu.SemaphoreType.DMA((PARTS,))]
        + ([pltpu.VMEM((total, columns), jnp.bfloat16)] if len(pieces) > 1 else []),
        cost_estimate=pl.CostEstimate(
            flops=2 * TERMS * out_rows * total * columns, bytes_accessed=2 * columns * (total + out_rows), transcendentals=0
        ),
        compiler_params=pltpu.CompilerParams(vmem_limit_bytes=(4 * total + 16 * out_rows) * columns + (4 << 20)),
        name="rebuild",
    )(matrix, *pieces)


def in_terms(x):
    terms = []
    for _ in range(TERMS):
        terms.append(lax.reduce_precision(x, 8, 7))
        x = x - terms[-1]
    return jnp.concatenate(terms, 0).astype(jnp.bfloat16)


def repair_matrix(decode_block, pair_block, recouple_pairs, sources, peers):
    stripes_here, helpers, plane_count = pair_block.shape
    group_size = decode_block.shape[1]
    helper_ids = jnp.arange(helpers, dtype=jnp.int32)
    choose = (pair_block[..., None] == helper_ids).astype(jnp.float32)
    coupled = (pair_block != helper_ids[None, :, None]).astype(jnp.float32)
    unmix = (jnp.eye(helpers, dtype=jnp.float32)[None, :, None, :] - COUPLING * coupled[..., None] * choose) / (
        1.0 - COUPLING * COUPLING
    )
    sectioned = jnp.einsum("sth,shzg->sztg", decode_block, unmix, precision=HIGHEST)
    sub_count = plane_count * group_size
    rows_in = jnp.arange(peers.shape[0] * plane_count, dtype=jnp.int32)
    peer_of_row = jnp.repeat(peers, plane_count)
    at_row = (sources.reshape(stripes_here, helpers)[..., None] == peer_of_row).astype(jnp.float32)
    spread = jnp.einsum(
        "sag,sgr->sar", sectioned.reshape(stripes_here, sub_count, helpers), at_row, precision=HIGHEST
    )
    same_plane = jnp.arange(sub_count, dtype=jnp.int32)[:, None] // group_size == rows_in[None, :] % plane_count
    spread = jnp.where(same_plane[None], spread, 0.0)
    sub_ids = jnp.arange(sub_count, dtype=jnp.int32)
    pick = (recouple_pairs[..., None] == sub_ids).astype(jnp.float32)
    distinct = (recouple_pairs != sub_ids[None, :]).astype(jnp.float32)
    mixing = jnp.eye(sub_count, dtype=jnp.float32)[None] + COUPLING * distinct[..., None] * pick
    whole = jnp.einsum("sab,sbc->sac", mixing, spread, precision=HIGHEST)
    return whole.reshape(stripes_here * sub_count, peers.shape[0] * plane_count)


def swap(x, mask, device_count):
    return lax.ppermute(x, AXES, [(q, q ^ mask) for q in range(device_count)])


def body(span_store, helper_offset, plane_index, coupling_pair, decode_matrix, recouple_pair):
    rack_count, dev_count = lax.axis_size("rack"), lax.axis_size("dev")
    device_count = rack_count * dev_count
    me = lax.axis_index("rack") * dev_count + lax.axis_index("dev")
    columns = span_store.shape[-1]
    stripes_here, helpers, plane_count = coupling_pair.shape
    sub_count = recouple_pair.shape[1]
    near = near_masks(rack_count)
    ahead = ahead_chips(rack_count, dev_count)
    rules = outgoing_rules(near, ahead, rack_count, dev_count)
    outgoing = pick_rows(rules, helpers, device_count, helper_offset, plane_index.T, span_store)
    across = [swap(x, m * dev_count, device_count) for m, x in zip(near, outgoing)]
    groups = None
    if rack_count > 1:
        groups = [
            [rack * dev_count + d for d in range(dev_count) for rack in (r, rack_count - 1 - r)]
            for r in range(rack_count // 2)
        ]
    blocks = put_in_hbm(outgoing[-1]).reshape(-1, plane_count, columns)
    far = lax.all_to_all(blocks, AXES, 0, 0, axis_index_groups=groups, tiled=True).reshape(-1, columns)
    peers = [far_peer(me, i, rack_count, dev_count) for i in range(far.shape[0] // plane_count)]
    arrived, counts = [far], [far.shape[0]]
    if near:
        chips = range(dev_count // 2)
        straight = [
            swap(x, near[0] * dev_count + 2 * chip, device_count)
            for chip, x in zip(ahead, outgoing[len(near) :])
        ]
        home = [(x, m * dev_count, 0) for m, x in zip(near, across)]
        home += [(x, near[0] * dev_count + 2 * chip, 0) for chip, x in zip(ahead, straight)]
        onward = [
            [(x, m * dev_count + 2 * chip, chip) for m, x in zip(near, across) if m != near[0] or chip not in ahead]
            for chip in chips[1:]
        ]

        def block(x, index):
            return x[index * plane_count : (index + 1) * plane_count]

        crossing = [block(x, 2 * chip + 1) for x, _, chip in home + sum(onward, [])]
        crossed = swap(jnp.concatenate(crossing, 0), 1, device_count)
        arrived += [x for x, _, _ in home] + [crossed]
        counts += [plane_count] * len(home) + [len(home) * plane_count]
        peers += [me ^ mask for _, mask, _ in home] + [me ^ mask ^ 1 for _, mask, _ in home]
        at = len(home) * plane_count
        for chip, some in zip(chips[1:], onward):
            size = len(some) * plane_count
            part = [block(x, 2 * chip) for x, _, _ in some] + [crossed[at : at + size]]
            arrived.append(swap(jnp.concatenate(part, 0), 2 * chip, device_count))
            counts.append(2 * size)
            peers += [me ^ mask ^ core for core in (0, 1) for _, mask, _ in some]
            at += size
    sources = (me + helper_offset) % device_count
    peers = jnp.stack([jnp.asarray(p, jnp.int32) for p in peers])
    whole = in_terms(repair_matrix(decode_matrix, coupling_pair, recouple_pair, sources, peers))
    return rebuild(whole, arrived, counts).reshape(stripes_here, sub_count, columns)


def solution(mesh):
    split = ("rack", "dev")
    placed = (
        P(split, None, None),
        P(),
        P(),
        P(split, None, None),
        P(split, None, None),
        P(split, None),
    )
    return jax.shard_map(body, mesh=mesh, in_specs=placed, out_specs=P(split, None, None), check_vma=False)
```

time: 49.5 us -> 47.7 us (0.964)
  starting transfers between devices: 16.5 us -> 21.1 us
  waiting for transfers between devices: 23.3 us -> 19.8 us
  Pallas kernels: 7.24 us -> 4.52 us
    ppermute x6 -> x8, starting transfers between devices: 8.09 us -> 12.7 us  [swap(): return lax.ppermute(x, AXES, [(q, q ^ mask) for q in range(device_count)])]
    ppermute x6 -> x8, waiting for transfers between devices: 23.3 us -> 19.8 us  [swap(): return lax.ppermute(x, AXES, [(q, q ^ mask) for q in range(device_count)])]
    pallas_call x2, Pallas kernels: 5.96 us -> 3.27 us  [the longest x1 2.46 us: pick_rows(): pl.pallas_call(functools.partial(pick_kernel, rules, helpers), out_shape=...]
  transfers between devices with their start and end apart: 7 -> 9, of which waited for: 4 -> 4; matrix products, arithmetic and copies ran while one was open for 4% -> 4% of each run, Pallas kernels for 5% -> 0%
where the time goes in v1:
time: 47.7 us; the launch traced here: 47.5 us
  starting transfers between devices  21.1 us (44%)
  waiting for transfers between devices  19.8 us (42%)
  Pallas kernels  4.52 us (9%)
  matrix products  1.07 us (2%)
  local copies, waits for them, and re-layouts  0.55 us (1%)
    ppermute x8, waiting for transfers between devices, swap(): return lax.ppermute(x, AXES, [(q, q ^ mask) for q in range(device_count)])  19.8 us
    ppermute x8, starting transfers between devices, swap(): return lax.ppermute(x, AXES, [(q, q ^ mask) for q in range(device_count)])  12.7 us
    all_to_all x1, starting transfers between devices, body(): lax.all_to_all(blocks, AXES, 0, 0, axis_index_groups=groups, tiled=True)  8.36 us
    pallas_call x1, Pallas kernels, pick_rows(): pl.pallas_call(functools.partial(pick_kernel, rules, helpers), out_shape=...  2.46 us
    pallas_call x1, Pallas kernels, rebuild(): pl.pallas_call(functools.partial(rebuild_kernel, counts), out_shape=jax.S...  1.25 us
  transfers between devices with their start and end apart: 9, of which 4 were waited for; matrix products, arithmetic and copies ran while one was open for 4% of the time, Pallas kernels for 0%

profile of v1, /device:TPU:0, one launch (start us, length us, event | category | flops | bytes accessed | tf_op | source)
XLA Modules:
  0.0 47.5 jit_solution(11321677201594892635)
XLA Ops:
  0.0 2.5 %pick_rows.1 = (bf16[64,1024]{1,0:T(8,128)(2,1)S(1)}, bf16[128,1024]{1,0:T(8,128)(2,1)S(1)}, bf16[32,1024]{1,0:T(8,128)(2,1)S(1)}, bf16[32,1024]{1,0:T(8,128)(2,1)S(1)}, bf16[256,1024]{1,0:T(8,128)(2,1)S(1)}) custom-call(s32[22]{0:T(128)} %offset_hbm.1, s32[16,64]{1,0:T(8,128)} %bitcast.55, bf16[22,64,1024]{2,1,0:T(8,128)(2,1)} %store_ref.1), custom_call_target="tpu_custom_call" | custom-call | flops 46137344 | bytes 3932160 | tf_op jit(solution)/shard_map/pick_rows/pallas_call | solution.py:99
  2.5 0.8 %put_in_hbm.1 = bf16[256,1024]{1,0:T(8,128)(2,1)} custom-call(bf16[256,1024]{1,0:T(8,128)(2,1)S(1)} %get-tuple-element.10.rows_ref), custom_call_target="tpu_custom_call" | custom-call | bytes 1048576 | tf_op jit(solution)/shard_map/put_in_hbm/pallas_call | solution.py:132
  3.3 8.4 %all-to-all-start = ((bf16[16,16,1024]{2,1,0:T(8,128)(2,1)}), bf16[16,16,1024]{2,1,0:T(8,128)(2,1)S(1)}, u32[]{:S(2)}, u32[]{:S(2)}) async-start(bf16[16,16,1024]{2,1,0:T(8,128)(2,1)} %bitcast.38), calls=%async_computation | async-start | bytes 1048576 | tf_op jit(solution)/shard_map/all_to_all | solution.py:245
  11.7 1.8 %collective-permute-start.2 = (bf16[32,1024]{1,0:T(8,128)(2,1)S(1)}, bf16[32,1024]{1,0:T(8,128)(2,1)S(1)}, u32[]{:S(2)}, u32[]{:S(2)}) collective-permute-start(bf16[32,1024]{1,0:T(8,128)(2,1)S(1)} %get-tuple-element.13), channel_id=1, source_target_pairs={{0,20},{1,21},{2,22},{3,23},{4,16},{5,17},{6,18},{7,19},{8,28},{9,... | collective-permute-start | bytes 196616 | tf_op jit(solution)/shard_map/ppermute | solution.py:223
  13.5 3.4 %collective-permute-start.3 = (bf16[32,1024]{1,0:T(8,128)(2,1)S(1)}, bf16[32,1024]{1,0:T(8,128)(2,1)S(1)}, u32[]{:S(2)}, u32[]{:S(2)}) collective-permute-start(bf16[32,1024]{1,0:T(8,128)(2,1)S(1)} %get-tuple-element.14), channel_id=1, source_target_pairs={{0,22},{1,23},{2,20},{3,21},{4,18},{5,19},{6,16},{7,17},{8,30},{9,... | collective-permute-start | bytes 196616 | tf_op jit(solution)/shard_map/ppermute | solution.py:223
  16.9 0.5 collective-permute-start
  17.3 3.4 %collective-permute-start.1 = (bf16[128,1024]{1,0:T(8,128)(2,1)S(1)}, bf16[128,1024]{1,0:T(8,128)(2,1)S(1)}, u32[]{:S(2)}, u32[]{:S(2)}) collective-permute-start(bf16[128,1024]{1,0:T(8,128)(2,1)S(1)} %get-tuple-element.12), channel_id=1, source_target_pairs={{0,8},{1,9},{2,10},{3,11},{4,12},{5,13},{6,14},{7,15},{8,0},{9,1},... | collective-permute-start | bytes 786440 | tf_op jit(solution)/shard_map/ppermute | solution.py:223
  20.8 0.1 eq.89
  20.9 0.1 stack.131
  21.1 0.1 eq.91
  21.1 0.3 convolution_bitcast_fusion
  21.5 0.1 copy.11
  21.6 0.1 broadcast_compare_fusion
  21.7 0.3 convolution_select_fusion
  22.1 14.2 %collective-permute-done.refs_1_ = bf16[64,1024]{1,0:T(8,128)(2,1)S(1)} collective-permute-done((bf16[64,1024]{1,0:T(8,128)(2,1)S(1)}, bf16[64,1024]{1,0:T(8,128)(2,1)S(1)}, u32[]{:S(2)}, u32[]{:S(2)}) %collective-permute-start) | collective-permute-done | bytes 131104 | tf_op jit(solution)/shard_map/ppermute | solution.py:223
  36.3 0.1 collective-permute-start.4
  36.4 0.4 fusion.10
  36.9 1.0 %collective-permute-done.4.refs_5_ = bf16[128,1024]{1,0:T(8,128)(2,1)S(1)} collective-permute-done((bf16[128,1024]{1,0:T(8,128)(2,1)S(1)}, bf16[128,1024]{1,0:T(8,128)(2,1)S(1)}, u32[]{:S(2)}, u32[]{:S(2)}) %collective-permute-start.4) | collective-permute-done | bytes 262176 | tf_op jit(solution)/shard_map/ppermute | solution.py:223
  38.0 1.5 %collective-permute-start.6 = (bf16[32,1024]{1,0:T(8,128)(2,1)S(1)}, bf16[32,1024]{1,0:T(8,128)(2,1)S(1)}, u32[]{:S(2)}, u32[]{:S(2)}) collective-permute-start(bf16[32,1024]{1,0:T(8,128)(2,1)S(1)} %pad_maximum_fusion.2), channel_id=1, source_target_pairs={{0,4},{1,5},{2,6},{3,7},{4,0},{5,1},{6,2},{7,3},{8,12},{9,13},{10,... | collective-permute-start | bytes 196616 | tf_op jit(solution)/shard_map/ppermute | solution.py:223
  39.5 1.5 %collective-permute-start.5 = (bf16[64,1024]{1,0:T(8,128)(2,1)S(1)}, bf16[64,1024]{1,0:T(8,128)(2,1)S(1)}, u32[]{:S(2)}, u32[]{:S(2)}) collective-permute-start(bf16[64,1024]{1,0:T(8,128)(2,1)S(1)} %pad_maximum_fusion.1), channel_id=1, source_target_pairs={{0,2},{1,3},{2,0},{3,1},{4,6},{5,7},{6,4},{7,5},{8,10},{9,11},{10,... | collective-permute-start | bytes 393224 | tf_op jit(solution)/shard_map/ppermute | solution.py:223
  41.0 0.6 %collective-permute-start.7 = (bf16[32,1024]{1,0:T(8,128)(2,1)S(1)}, bf16[32,1024]{1,0:T(8,128)(2,1)S(1)}, u32[]{:S(2)}, u32[]{:S(2)}) collective-permute-start(bf16[32,1024]{1,0:T(8,128)(2,1)S(1)} %pad_maximum_fusion.3), channel_id=1, source_target_pairs={{0,6},{1,7},{2,4},{3,5},{4,2},{5,3},{6,0},{7,1},{8,14},{9,15},{10,... | collective-permute-start | bytes 196616 | tf_op jit(solution)/shard_map/ppermute | solution.py:223
  41.6 0.7 %collective-permute-done.6.refs_7_ = bf16[32,1024]{1,0:T(8,128)(2,1)S(1)} collective-permute-done((bf16[32,1024]{1,0:T(8,128)(2,1)S(1)}, bf16[32,1024]{1,0:T(8,128)(2,1)S(1)}, u32[]{:S(2)}, u32[]{:S(2)}) %collective-permute-start.6) | collective-permute-done | bytes 65568 | tf_op jit(solution)/shard_map/ppermute | solution.py:223
  42.3 3.9 %collective-permute-done.7.refs_8_ = bf16[32,1024]{1,0:T(8,128)(2,1)S(1)} collective-permute-done((bf16[32,1024]{1,0:T(8,128)(2,1)S(1)}, bf16[32,1024]{1,0:T(8,128)(2,1)S(1)}, u32[]{:S(2)}, u32[]{:S(2)}) %collective-permute-start.7) | collective-permute-done | bytes 65568 | tf_op jit(solution)/shard_map/ppermute | solution.py:223
  46.2 1.3 %rebuild.1 = bf16[128,1024]{1,0:T(8,128)(2,1)} custom-call(bf16[384,512]{1,0:T(8,128)(2,1)S(1)} %pad_maximum_fusion.matrix_ref, bf16[256,1024]{1,0:T(8,128)(2,1)S(1)} %bitcast.53, bf16[64,1024]{1,0:T(8,128)(2,1)S(1)} %collective-permute-done.refs_1_, bf16[128,1024]{1,0:T(8,128)(2,1)S(1)} %collective-permute-done.1.refs_2_, ...), custom_call_target="tpu_custom_call" | custom-call | flops 402653184 | bytes 1310720 | tf_op jit(solution)/shard_map/rebuild/pallas_call | solution.py:172
  (38 shorter events, 0.3 us)
Async XLA Ops:
  0.0 21.1 %copy-start = (f32[2,4,11]{2,1,0:T(4,128)S(1)}, f32[2,4,11]{2,1,0:T(4,128)}, u32[]{:S(2)}) copy-start(f32[2,4,11]{2,1,0:T(4,128)} %param.10) | copy-start | bytes 1060
  0.0 20.7 %copy-start.3 = (s32[22]{0:T(128)S(1)}, s32[22]{0:T(128)}, u32[]{:S(2)}) copy-start(s32[22]{0:T(128)} %offset_hbm.1) | copy-start | bytes 268
  0.0 20.7 %copy-start.1 = (s32[2,11,16]{2,0,1:T(2,128)S(1)}, s32[2,11,16]{2,0,1:T(2,128)}, u32[]{:S(2)}) copy-start(s32[2,11,16]{2,0,1:T(2,128)} %param.9) | copy-start | bytes 4228
  0.0 22.0 %copy-start.2 = (s32[2,64]{1,0:T(2,128)S(1)}, s32[2,64]{1,0:T(2,128)}, u32[]{:S(2)}) copy-start(s32[2,64]{1,0:T(2,128)} %param.11) | copy-start | bytes 1540
  3.3 42.9 %all-to-all-start = ((bf16[16,16,1024]{2,1,0:T(8,128)(2,1)}), bf16[16,16,1024]{2,1,0:T(8,128)(2,1)S(1)}, u32[]{:S(2)}, u32[]{:S(2)}) async-start(bf16[16,16,1024]{2,1,0:T(8,128)(2,1)} %bitcast.38), calls=%async_computation | async-start | bytes 1048576 | tf_op jit(solution)/shard_map/all_to_all | solution.py:245
  11.7 24.6 %collective-permute-start.2 = (bf16[32,1024]{1,0:T(8,128)(2,1)S(1)}, bf16[32,1024]{1,0:T(8,128)(2,1)S(1)}, u32[]{:S(2)}, u32[]{:S(2)}) collective-permute-start(bf16[32,1024]{1,0:T(8,128)(2,1)S(1)} %get-tuple-element.13), channel_id=1, source_target_pairs={{0,20},{1,21},{2,22},{3,23},{4,16},{5,17},{6,18},{7,19},{8,28},{9,... | collective-permute-start | bytes 196616 | tf_op jit(solution)/shard_map/ppermute | solution.py:223
  13.5 22.8 %collective-permute-start.3 = (bf16[32,1024]{1,0:T(8,128)(2,1)S(1)}, bf16[32,1024]{1,0:T(8,128)(2,1)S(1)}, u32[]{:S(2)}, u32[]{:S(2)}) collective-permute-start(bf16[32,1024]{1,0:T(8,128)(2,1)S(1)} %get-tuple-element.14), channel_id=1, source_target_pairs={{0,22},{1,23},{2,20},{3,21},{4,18},{5,19},{6,16},{7,17},{8,30},{9,... | collective-permute-start | bytes 196616 | tf_op jit(solution)/shard_map/ppermute | solution.py:223
  16.9 19.4 %collective-permute-start = (bf16[64,1024]{1,0:T(8,128)(2,1)S(1)}, bf16[64,1024]{1,0:T(8,128)(2,1)S(1)}, u32[]{:S(2)}, u32[]{:S(2)}) collective-permute-start(bf16[64,1024]{1,0:T(8,128)(2,1)S(1)} %get-tuple-element.11), channel_id=1, source_target_pairs={{0,16},{1,17},{2,18},{3,19},{4,20},{5,21},{6,22},{7,23},{8,24},{9,... | collective-permute-start | bytes 393224 | tf_op jit(solution)/shard_map/ppermute | solution.py:223
  17.3 18.9 %collective-permute-start.1 = (bf16[128,1024]{1,0:T(8,128)(2,1)S(1)}, bf16[128,1024]{1,0:T(8,128)(2,1)S(1)}, u32[]{:S(2)}, u32[]{:S(2)}) collective-permute-start(bf16[128,1024]{1,0:T(8,128)(2,1)S(1)} %get-tuple-element.12), channel_id=1, source_target_pairs={{0,8},{1,9},{2,10},{3,11},{4,12},{5,13},{6,14},{7,15},{8,0},{9,1},... | collective-permute-start | bytes 786440 | tf_op jit(solution)/shard_map/ppermute | solution.py:223
  36.3 1.6 %collective-permute-start.4 = (bf16[128,1024]{1,0:T(8,128)(2,1)S(1)}, bf16[128,1024]{1,0:T(8,128)(2,1)S(1)}, u32[]{:S(2)}, u32[]{:S(2)}) collective-permute-start(bf16[128,1024]{1,0:T(8,128)(2,1)S(1)} %get-tuple-element.18), channel_id=1, source_target_pairs={{0,1},{1,0},{2,3},{3,2},{4,5},{5,4},{6,7},{7,6},{8,9},{9,8},{10,11... | collective-permute-start | bytes 786440 | tf_op jit(solution)/shard_map/ppermute | solution.py:223
  38.0 4.3 %collective-permute-start.6 = (bf16[32,1024]{1,0:T(8,128)(2,1)S(1)}, bf16[32,1024]{1,0:T(8,128)(2,1)S(1)}, u32[]{:S(2)}, u32[]{:S(2)}) collective-permute-start(bf16[32,1024]{1,0:T(8,128)(2,1)S(1)} %pad_maximum_fusion.2), channel_id=1, source_target_pairs={{0,4},{1,5},{2,6},{3,7},{4,0},{5,1},{6,2},{7,3},{8,12},{9,13},{10,... | collective-permute-start | bytes 196616 | tf_op jit(solution)/shard_map/ppermute | solution.py:223
  39.5 6.7 %collective-permute-start.5 = (bf16[64,1024]{1,0:T(8,128)(2,1)S(1)}, bf16[64,1024]{1,0:T(8,128)(2,1)S(1)}, u32[]{:S(2)}, u32[]{:S(2)}) collective-permute-start(bf16[64,1024]{1,0:T(8,128)(2,1)S(1)} %pad_maximum_fusion.1), channel_id=1, source_target_pairs={{0,2},{1,3},{2,0},{3,1},{4,6},{5,7},{6,4},{7,5},{8,10},{9,11},{10,... | collective-permute-start | bytes 393224 | tf_op jit(solution)/shard_map/ppermute | solution.py:223
  41.0 5.2 %collective-permute-start.7 = (bf16[32,1024]{1,0:T(8,128)(2,1)S(1)}, bf16[32,1024]{1,0:T(8,128)(2,1)S(1)}, u32[]{:S(2)}, u32[]{:S(2)}) collective-permute-start(bf16[32,1024]{1,0:T(8,128)(2,1)S(1)} %pad_maximum_fusion.3), channel_id=1, source_target_pairs={{0,6},{1,7},{2,4},{3,5},{4,2},{5,3},{6,0},{7,1},{8,14},{9,15},{10,... | collective-permute-start | bytes 196616 | tf_op jit(solution)/shard_map/ppermute | solution.py:223

commit v2 on v1

--- a/solution.py
+++ b/solution.py
@@ -141,23 +141,39 @@
     )(rows)
 
 
-def rebuild_kernel(counts, matrix_ref, *refs):
-    rows_refs, (out_ref, made, store_sem, *scratch) = refs[: len(counts)], refs[len(counts) :]
-    out_rows = out_ref.shape[0]
-    rows = rows_refs[0]
-    if len(counts) > 1:
-        rows, at = scratch[0], 0
-        for r, count in zip(rows_refs, counts):
-            rows[pl.ds(at, count)] = r[pl.ds(0, count)]
-            at += count
-    wide = out_ref.shape[1] // PARTS
+def gather_rows(scratch, rows_refs, counts):
+    at = 0
+    for r, count in zip(rows_refs, counts):
+        scratch[pl.ds(at, count)] = r[pl.ds(0, count)]
+        at += count
+
+
+def add_terms(terms, out_rows):
+    total = terms[:out_rows]
+    for t in range(1, TERMS):
+        total += terms[t * out_rows : (t + 1) * out_rows]
+    return total
+
+
+def begin_kernel(counts, matrix_ref, *refs):
+    rows_refs, (out_ref, rows) = refs[: len(counts)], refs[len(counts) :]
+    gather_rows(rows, rows_refs, counts)
+    terms = jnp.dot(matrix_ref[:, : rows.shape[0]], rows[...], preferred_element_type=jnp.float32)
+    out_ref[...] = add_terms(terms, out_ref.shape[0])
+
+
+def finish_kernel(counts, skip, matrix_ref, begun_ref, *refs):
+    rows_refs, (out_ref, made, rows, store_sem) = refs[: len(counts)], refs[len(counts) :]
+    out_rows, columns = out_ref.shape
+    gather_rows(rows, rows_refs, counts)
+    wide = columns // PARTS
     stores = []
     for c in range(PARTS):
         part = pl.ds(c * wide, wide)
-        terms = jnp.dot(matrix_ref[...], rows[:, part], preferred_element_type=jnp.float32)
-        total = terms[:out_rows]
-        for t in range(1, TERMS):
-            total += terms[t * out_rows : (t + 1) * out_rows]
+        total = begun_ref[:, part]
+        if counts:
+            terms = jnp.dot(matrix_ref[:, skip:], rows[:, part], preferred_element_type=jnp.float32)
+            total += add_terms(terms, out_rows)
         made[:, part] = total.astype(made.dtype)
         stores.append(pltpu.make_async_copy(made.at[:, part], out_ref.at[:, part], store_sem.at[c]))
         stores[-1].start()
@@ -165,23 +181,45 @@
         copy.wait()
 
 
-def rebuild(matrix, pieces, counts):
+def rebuild(matrix, pieces, counts, split):
     out_rows = matrix.shape[0] // TERMS
     columns = pieces[0].shape[1]
-    total = sum(counts)
+    early, late = sum(counts[:split]), sum(counts[split:])
+
+    def settings(rows):
+        return dict(
+            cost_estimate=pl.CostEstimate(
+                flops=2 * TERMS * out_rows * rows * columns,
+                bytes_accessed=2 * columns * (rows + out_rows),
+                transcendentals=0,
+            ),
+            compiler_params=pltpu.CompilerParams(
+                vmem_limit_bytes=(4 * rows + 16 * out_rows) * columns + 4 * matrix.size + (4 << 20)
+            ),
+        )
+
+    begun = pl.pallas_call(
+        functools.partial(begin_kernel, counts[:split]),
+        out_shape=jax.ShapeDtypeStruct((out_rows, columns), jnp.float32),
+        in_specs=[VMEM] * (1 + split),
+        out_specs=VMEM,
+        scratch_shapes=[pltpu.VMEM((early, columns), jnp.bfloat16)],
+        name="begin",
+        **settings(early),
+    )(matrix, *pieces[:split])
     return pl.pallas_call(
-        functools.partial(rebuild_kernel, counts),
+        functools.partial(finish_kernel, counts[split:], early),
         out_shape=jax.ShapeDtypeStruct((out_rows, columns), jnp.bfloat16),
-        in_specs=[VMEM] * (1 + len(pieces)),
+        in_specs=[VMEM] * (2 + len(pieces) - split),
         out_specs=HBM,
-        scratch_shapes=[pltpu.VMEM((out_rows, columns), jnp.bfloat16), pltpu.SemaphoreType.DMA((PARTS,))]
-        + ([pltpu.VMEM((total, columns), jnp.bfloat16)] if len(pieces) > 1 else []),
-        cost_estimate=pl.CostEstimate(
-            flops=2 * TERMS * out_rows * total * columns, bytes_accessed=2 * columns * (total + out_rows), transcendentals=0
-        ),
-        compiler_params=pltpu.CompilerParams(vmem_limit_bytes=(4 * total + 16 * out_rows) * columns + (4 << 20)),
-        name="rebuild",
-    )(matrix, *pieces)
+        scratch_shapes=[
+            pltpu.VMEM((out_rows, columns), jnp.bfloat16),
+            pltpu.VMEM((max(late, 16), columns), jnp.bfloat16),
+            pltpu.SemaphoreType.DMA((PARTS,)),
+        ],
+        name="finish",
+        **settings(late),
+    )(matrix, begun, *pieces[split:])
 
 
 def in_terms(x):
@@ -274,10 +312,11 @@
             counts.append(2 * size)
             peers += [me ^ mask ^ core for core in (0, 1) for _, mask, _ in some]
             at += size
+    split = len(arrived) - (dev_count // 2 - 1 if near else 0)
     sources = (me + helper_offset) % device_count
     peers = jnp.stack([jnp.asarray(p, jnp.int32) for p in peers])
     whole = in_terms(repair_matrix(decode_matrix, coupling_pair, recouple_pair, sources, peers))
-    return rebuild(whole, arrived, counts).reshape(stripes_here, sub_count, columns)
+    return rebuild(whole, arrived, counts, split).reshape(stripes_here, sub_count, columns)
 
 
 def solution(mesh):

time: 47.7 us -> 47.8 us (level)
    pallas_call x1 -> x2, Pallas kernels: 1.25 us -> 1.59 us  [the longest x1 1.03 us: rebuild(): pl.pallas_call(functools.partial(finish_kernel, counts[split:], early), o...]
  transfers between devices with their start and end apart: 9 -> 9, of which waited for: 4 -> 5; matrix products, arithmetic and copies ran while one was open for 4% -> 4% of each run, Pallas kernels for 0% -> 1%
where the time goes in v2:
time: 47.8 us; the launch traced here: 47.6 us
  starting transfers between devices  21.1 us (44%)
  waiting for transfers between devices  19.5 us (41%)
  Pallas kernels  4.86 us (10%)
  matrix products  1.07 us (2%)
  local copies, waits for them, and re-layouts  0.55 us (1%)
    ppermute x8, waiting for transfers between devices, swap(): return lax.ppermute(x, AXES, [(q, q ^ mask) for q in range(device_count)])  19.5 us
    ppermute x8, starting transfers between devices, swap(): return lax.ppermute(x, AXES, [(q, q ^ mask) for q in range(device_count)])  12.7 us
    all_to_all x1, starting transfers between devices, body(): lax.all_to_all(blocks, AXES, 0, 0, axis_index_groups=groups, tiled=True)  8.36 us
    pallas_call x1, Pallas kernels, pick_rows(): pl.pallas_call(functools.partial(pick_kernel, rules, helpers), out_shape=...  2.46 us
    pallas_call x1, Pallas kernels, rebuild(): pl.pallas_call(functools.partial(finish_kernel, counts[split:], early), o...  1.03 us
  transfers between devices with their start and end apart: 9, of which 5 were waited for; matrix products, arithmetic and copies ran while one was open for 4% of the time, Pallas kernels for 1%

profile of v2, /device:TPU:0, one launch (start us, length us, event | category | flops | bytes accessed | tf_op | source)
XLA Modules:
  0.0 47.6 jit_solution(12643838016385125259)
XLA Ops:
  0.0 2.5 %pick_rows.1 = (bf16[64,1024]{1,0:T(8,128)(2,1)S(1)}, bf16[128,1024]{1,0:T(8,128)(2,1)S(1)}, bf16[32,1024]{1,0:T(8,128)(2,1)S(1)}, bf16[32,1024]{1,0:T(8,128)(2,1)S(1)}, bf16[256,1024]{1,0:T(8,128)(2,1)S(1)}) custom-call(s32[22]{0:T(128)} %offset_hbm.1, s32[16,64]{1,0:T(8,128)} %bitcast.55, bf16[22,64,1024]{2,1,0:T(8,128)(2,1)} %store_ref.1), custom_call_target="tpu_custom_call" | custom-call | flops 46137344 | bytes 3932160 | tf_op jit(solution)/shard_map/pick_rows/pallas_call | solution.py:99
  2.5 0.8 %put_in_hbm.1 = bf16[256,1024]{1,0:T(8,128)(2,1)} custom-call(bf16[256,1024]{1,0:T(8,128)(2,1)S(1)} %get-tuple-element.10.rows_ref), custom_call_target="tpu_custom_call" | custom-call | bytes 1048576 | tf_op jit(solution)/shard_map/put_in_hbm/pallas_call | solution.py:132
  3.3 8.4 %all-to-all-start = ((bf16[16,16,1024]{2,1,0:T(8,128)(2,1)}), bf16[16,16,1024]{2,1,0:T(8,128)(2,1)S(1)}, u32[]{:S(2)}, u32[]{:S(2)}) async-start(bf16[16,16,1024]{2,1,0:T(8,128)(2,1)} %bitcast.38), calls=%async_computation | async-start | bytes 1048576 | tf_op jit(solution)/shard_map/all_to_all | solution.py:283
  11.7 1.8 %collective-permute-start.2 = (bf16[32,1024]{1,0:T(8,128)(2,1)S(1)}, bf16[32,1024]{1,0:T(8,128)(2,1)S(1)}, u32[]{:S(2)}, u32[]{:S(2)}) collective-permute-start(bf16[32,1024]{1,0:T(8,128)(2,1)S(1)} %get-tuple-element.13), channel_id=1, source_target_pairs={{0,20},{1,21},{2,22},{3,23},{4,16},{5,17},{6,18},{7,19},{8,28},{9,... | collective-permute-start | bytes 196616 | tf_op jit(solution)/shard_map/ppermute | solution.py:261
  13.5 3.4 %collective-permute-start.3 = (bf16[32,1024]{1,0:T(8,128)(2,1)S(1)}, bf16[32,1024]{1,0:T(8,128)(2,1)S(1)}, u32[]{:S(2)}, u32[]{:S(2)}) collective-permute-start(bf16[32,1024]{1,0:T(8,128)(2,1)S(1)} %get-tuple-element.14), channel_id=1, source_target_pairs={{0,22},{1,23},{2,20},{3,21},{4,18},{5,19},{6,16},{7,17},{8,30},{9,... | collective-permute-start | bytes 196616 | tf_op jit(solution)/shard_map/ppermute | solution.py:261
  16.9 0.5 collective-permute-start
  17.3 3.4 %collective-permute-start.1 = (bf16[128,1024]{1,0:T(8,128)(2,1)S(1)}, bf16[128,1024]{1,0:T(8,128)(2,1)S(1)}, u32[]{:S(2)}, u32[]{:S(2)}) collective-permute-start(bf16[128,1024]{1,0:T(8,128)(2,1)S(1)} %get-tuple-element.12), channel_id=1, source_target_pairs={{0,8},{1,9},{2,10},{3,11},{4,12},{5,13},{6,14},{7,15},{8,0},{9,1},... | collective-permute-start | bytes 786440 | tf_op jit(solution)/shard_map/ppermute | solution.py:261
  20.8 0.1 eq.89
  20.9 0.1 stack.131
  21.1 0.1 eq.91
  21.1 0.3 convolution_bitcast_fusion
  21.5 0.1 copy.11
  21.6 0.1 broadcast_compare_fusion
  21.7 0.3 convolution_select_fusion
  22.1 14.2 %collective-permute-done.refs_1_ = bf16[64,1024]{1,0:T(8,128)(2,1)S(1)} collective-permute-done((bf16[64,1024]{1,0:T(8,128)(2,1)S(1)}, bf16[64,1024]{1,0:T(8,128)(2,1)S(1)}, u32[]{:S(2)}, u32[]{:S(2)}) %collective-permute-start) | collective-permute-done | bytes 131104 | tf_op jit(solution)/shard_map/ppermute | solution.py:261
  36.4 0.4 fusion.10
  36.9 1.0 %collective-permute-done.4.refs_5_ = bf16[128,1024]{1,0:T(8,128)(2,1)S(1)} collective-permute-done((bf16[128,1024]{1,0:T(8,128)(2,1)S(1)}, bf16[128,1024]{1,0:T(8,128)(2,1)S(1)}, u32[]{:S(2)}, u32[]{:S(2)}) %collective-permute-start.4) | collective-permute-done | bytes 262176 | tf_op jit(solution)/shard_map/ppermute | solution.py:261
  38.0 1.5 %collective-permute-start.6 = (bf16[32,1024]{1,0:T(8,128)(2,1)S(1)}, bf16[32,1024]{1,0:T(8,128)(2,1)S(1)}, u32[]{:S(2)}, u32[]{:S(2)}) collective-permute-start(bf16[32,1024]{1,0:T(8,128)(2,1)S(1)} %pad_maximum_fusion.2), channel_id=1, source_target_pairs={{0,4},{1,5},{2,6},{3,7},{4,0},{5,1},{6,2},{7,3},{8,12},{9,13},{10,... | collective-permute-start | bytes 196616 | tf_op jit(solution)/shard_map/ppermute | solution.py:261
  39.5 1.5 %collective-permute-start.7 = (bf16[32,1024]{1,0:T(8,128)(2,1)S(1)}, bf16[32,1024]{1,0:T(8,128)(2,1)S(1)}, u32[]{:S(2)}, u32[]{:S(2)}) collective-permute-start(bf16[32,1024]{1,0:T(8,128)(2,1)S(1)} %pad_maximum_fusion.3), channel_id=1, source_target_pairs={{0,6},{1,7},{2,4},{3,5},{4,2},{5,3},{6,0},{7,1},{8,14},{9,15},{10,... | collective-permute-start | bytes 196616 | tf_op jit(solution)/shard_map/ppermute | solution.py:261
  41.0 0.6 %collective-permute-start.5 = (bf16[64,1024]{1,0:T(8,128)(2,1)S(1)}, bf16[64,1024]{1,0:T(8,128)(2,1)S(1)}, u32[]{:S(2)}, u32[]{:S(2)}) collective-permute-start(bf16[64,1024]{1,0:T(8,128)(2,1)S(1)} %pad_maximum_fusion.1), channel_id=1, source_target_pairs={{0,2},{1,3},{2,0},{3,1},{4,6},{5,7},{6,4},{7,5},{8,10},{9,11},{10,... | collective-permute-start | bytes 393224 | tf_op jit(solution)/shard_map/ppermute | solution.py:261
  41.6 0.6 %begin.1.begun_ref = f32[128,1024]{1,0:T(8,128)S(1)} custom-call(bf16[384,512]{1,0:T(8,128)(2,1)S(1)} %pad_maximum_fusion.matrix_ref, bf16[256,1024]{1,0:T(8,128)(2,1)S(1)} %bitcast.53, bf16[64,1024]{1,0:T(8,128)(2,1)S(1)} %collective-permute-done.refs_1_, bf16[128,1024]{1,0:T(8,128)(2,1)S(1)} %collective-permute-done.1.refs_2_, ...), custom_call_target="tpu_custom_call" | custom-call | flops 301989888 | bytes 1048576 | tf_op jit(solution)/shard_map/begin/pallas_call | solution.py:201
  42.3 2.9 %collective-permute-done.7.refs_2_ = bf16[32,1024]{1,0:T(8,128)(2,1)S(1)} collective-permute-done((bf16[32,1024]{1,0:T(8,128)(2,1)S(1)}, bf16[32,1024]{1,0:T(8,128)(2,1)S(1)}, u32[]{:S(2)}, u32[]{:S(2)}) %collective-permute-start.7) | collective-permute-done | bytes 65568 | tf_op jit(solution)/shard_map/ppermute | solution.py:261
  45.2 1.4 %collective-permute-done.5.refs_0_ = bf16[64,1024]{1,0:T(8,128)(2,1)S(1)} collective-permute-done((bf16[64,1024]{1,0:T(8,128)(2,1)S(1)}, bf16[64,1024]{1,0:T(8,128)(2,1)S(1)}, u32[]{:S(2)}, u32[]{:S(2)}) %collective-permute-start.5) | collective-permute-done | bytes 131104 | tf_op jit(solution)/shard_map/ppermute | solution.py:261
  46.6 1.0 %finish.1 = bf16[128,1024]{1,0:T(8,128)(2,1)} custom-call(bf16[384,512]{1,0:T(8,128)(2,1)S(1)} %pad_maximum_fusion.matrix_ref, f32[128,1024]{1,0:T(8,128)S(1)} %begin.1.begun_ref, bf16[64,1024]{1,0:T(8,128)(2,1)S(1)} %collective-permute-done.5.refs_0_, bf16[32,1024]{1,0:T(8,128)(2,1)S(1)} %collective-permute-done.6.refs_1_, ...), custom_call_target="tpu_custom_call" | custom-call | flops 100663296 | bytes 524288 | tf_op jit(solution)/shard_map/finish/pallas_call | solution.py:210
  (39 shorter events, 0.5 us)
Async XLA Ops:
  0.0 21.1 %copy-start = (f32[2,4,11]{2,1,0:T(4,128)S(1)}, f32[2,4,11]{2,1,0:T(4,128)}, u32[]{:S(2)}) copy-start(f32[2,4,11]{2,1,0:T(4,128)} %param.10) | copy-start | bytes 1060
  0.0 20.7 %copy-start.3 = (s32[22]{0:T(128)S(1)}, s32[22]{0:T(128)}, u32[]{:S(2)}) copy-start(s32[22]{0:T(128)} %offset_hbm.1) | copy-start | bytes 268
  0.0 20.7 %copy-start.1 = (s32[2,11,16]{2,0,1:T(2,128)S(1)}, s32[2,11,16]{2,0,1:T(2,128)}, u32[]{:S(2)}) copy-start(s32[2,11,16]{2,0,1:T(2,128)} %param.9) | copy-start | bytes 4228
  0.0 22.0 %copy-start.2 = (s32[2,64]{1,0:T(2,128)S(1)}, s32[2,64]{1,0:T(2,128)}, u32[]{:S(2)}) copy-start(s32[2,64]{1,0:T(2,128)} %param.11) | copy-start | bytes 1540
  3.3 38.3 %all-to-all-start = ((bf16[16,16,1024]{2,1,0:T(8,128)(2,1)}), bf16[16,16,1024]{2,1,0:T(8,128)(2,1)S(1)}, u32[]{:S(2)}, u32[]{:S(2)}) async-start(bf16[16,16,1024]{2,1,0:T(8,128)(2,1)} %bitcast.38), calls=%async_computation | async-start | bytes 1048576 | tf_op jit(solution)/shard_map/all_to_all | solution.py:283
  11.7 24.6 %collective-permute-start.2 = (bf16[32,1024]{1,0:T(8,128)(2,1)S(1)}, bf16[32,1024]{1,0:T(8,128)(2,1)S(1)}, u32[]{:S(2)}, u32[]{:S(2)}) collective-permute-start(bf16[32,1024]{1,0:T(8,128)(2,1)S(1)} %get-tuple-element.13), channel_id=1, source_target_pairs={{0,20},{1,21},{2,22},{3,23},{4,16},{5,17},{6,18},{7,19},{8,28},{9,... | collective-permute-start | bytes 196616 | tf_op jit(solution)/shard_map/ppermute | solution.py:261
  13.5 22.8 %collective-permute-start.3 = (bf16[32,1024]{1,0:T(8,128)(2,1)S(1)}, bf16[32,1024]{1,0:T(8,128)(2,1)S(1)}, u32[]{:S(2)}, u32[]{:S(2)}) collective-permute-start(bf16[32,1024]{1,0:T(8,128)(2,1)S(1)} %get-tuple-element.14), channel_id=1, source_target_pairs={{0,22},{1,23},{2,20},{3,21},{4,18},{5,19},{6,16},{7,17},{8,30},{9,... | collective-permute-start | bytes 196616 | tf_op jit(solution)/shard_map/ppermute | solution.py:261
  16.9 19.4 %collective-permute-start = (bf16[64,1024]{1,0:T(8,128)(2,1)S(1)}, bf16[64,1024]{1,0:T(8,128)(2,1)S(1)}, u32[]{:S(2)}, u32[]{:S(2)}) collective-permute-start(bf16[64,1024]{1,0:T(8,128)(2,1)S(1)} %get-tuple-element.11), channel_id=1, source_target_pairs={{0,16},{1,17},{2,18},{3,19},{4,20},{5,21},{6,22},{7,23},{8,24},{9,... | collective-permute-start | bytes 393224 | tf_op jit(solution)/shard_map/ppermute | solution.py:261
  17.3 18.9 %collective-permute-start.1 = (bf16[128,1024]{1,0:T(8,128)(2,1)S(1)}, bf16[128,1024]{1,0:T(8,128)(2,1)S(1)}, u32[]{:S(2)}, u32[]{:S(2)}) collective-permute-start(bf16[128,1024]{1,0:T(8,128)(2,1)S(1)} %get-tuple-element.12), channel_id=1, source_target_pairs={{0,8},{1,9},{2,10},{3,11},{4,12},{5,13},{6,14},{7,15},{8,0},{9,1},... | collective-permute-start | bytes 786440 | tf_op jit(solution)/shard_map/ppermute | solution.py:261
  36.3 1.6 %collective-permute-start.4 = (bf16[128,1024]{1,0:T(8,128)(2,1)S(1)}, bf16[128,1024]{1,0:T(8,128)(2,1)S(1)}, u32[]{:S(2)}, u32[]{:S(2)}) collective-permute-start(bf16[128,1024]{1,0:T(8,128)(2,1)S(1)} %get-tuple-element.18), channel_id=1, source_target_pairs={{0,1},{1,0},{2,3},{3,2},{4,5},{5,4},{6,7},{7,6},{8,9},{9,8},{10,11... | collective-permute-start | bytes 786440 | tf_op jit(solution)/shard_map/ppermute | solution.py:261
  38.0 4.3 %collective-permute-start.6 = (bf16[32,1024]{1,0:T(8,128)(2,1)S(1)}, bf16[32,1024]{1,0:T(8,128)(2,1)S(1)}, u32[]{:S(2)}, u32[]{:S(2)}) collective-permute-start(bf16[32,1024]{1,0:T(8,128)(2,1)S(1)} %pad_maximum_fusion.2), channel_id=1, source_target_pairs={{0,4},{1,5},{2,6},{3,7},{4,0},{5,1},{6,2},{7,3},{8,12},{9,13},{10,... | collective-permute-start | bytes 196616 | tf_op jit(solution)/shard_map/ppermute | solution.py:261
  39.5 5.7 %collective-permute-start.7 = (bf16[32,1024]{1,0:T(8,128)(2,1)S(1)}, bf16[32,1024]{1,0:T(8,128)(2,1)S(1)}, u32[]{:S(2)}, u32[]{:S(2)}) collective-permute-start(bf16[32,1024]{1,0:T(8,128)(2,1)S(1)} %pad_maximum_fusion.3), channel_id=1, source_target_pairs={{0,6},{1,7},{2,4},{3,5},{4,2},{5,3},{6,0},{7,1},{8,14},{9,15},{10,... | collective-permute-start | bytes 196616 | tf_op jit(solution)/shard_map/ppermute | solution.py:261
  41.0 5.6 %collective-permute-start.5 = (bf16[64,1024]{1,0:T(8,128)(2,1)S(1)}, bf16[64,1024]{1,0:T(8,128)(2,1)S(1)}, u32[]{:S(2)}, u32[]{:S(2)}) collective-permute-start(bf16[64,1024]{1,0:T(8,128)(2,1)S(1)} %pad_maximum_fusion.1), channel_id=1, source_target_pairs={{0,2},{1,3},{2,0},{3,1},{4,6},{5,7},{6,4},{7,5},{8,10},{9,11},{10,... | collective-permute-start | bytes 393224 | tf_op jit(solution)/shard_map/ppermute | solution.py:261

commit v3 on v2

--- a/solution.py
+++ b/solution.py
@@ -13,7 +13,7 @@
 TOGETHER = 8
 AHEAD = 2
 TERMS = 3
-PARTS = 2
+PARTS = 1
 HBM = pl.BlockSpec(memory_space=pltpu.HBM)
 VMEM = pl.BlockSpec(memory_space=pltpu.VMEM)
 
@@ -122,10 +122,14 @@
     )(*(pltpu.with_memory_space_constraint(x, pltpu.HBM) for x in (helper_offset, planes, store)))
 
 
-def put_kernel(rows_ref, out_ref, sem):
-    copy = pltpu.make_async_copy(rows_ref, out_ref, sem)
-    copy.start()
-    copy.wait()
+def put_kernel(rows_ref, out_ref, sems):
+    size = rows_ref.shape[0] // sems.shape[0]
+    parts = [pl.ds(i * size, size) for i in range(sems.shape[0])]
+    copies = [pltpu.make_async_copy(rows_ref.at[p], out_ref.at[p], sems.at[i]) for i, p in enumerate(parts)]
+    for copy in copies:
+        copy.start()
+    for copy in copies:
+        copy.wait()
 
 
 def put_in_hbm(rows):
@@ -134,7 +138,7 @@
         out_shape=jax.ShapeDtypeStruct(rows.shape, rows.dtype),
         in_specs=[VMEM],
         out_specs=HBM,
-        scratch_shapes=[pltpu.SemaphoreType.DMA],
+        scratch_shapes=[pltpu.SemaphoreType.DMA((4,))],
         cost_estimate=pl.CostEstimate(flops=0, bytes_accessed=4 * rows.size, transcendentals=0),
         compiler_params=pltpu.CompilerParams(vmem_limit_bytes=2 * rows.size + (4 << 20)),
         name="put_in_hbm",

time: 47.8 us -> 47.9 us (level)
  no operation moved by 1% of the time
where the time goes in v3:
time: 47.9 us; the launch traced here: 47.7 us
  starting transfers between devices  21.1 us (44%)
  waiting for transfers between devices  19.6 us (41%)
  Pallas kernels  4.93 us (10%)
  matrix products  1.06 us (2%)
  local copies, waits for them, and re-layouts  0.55 us (1%)
    ppermute x8, waiting for transfers between devices, swap(): return lax.ppermute(x, AXES, [(q, q ^ mask) for q in range(device_count)])  19.6 us
    ppermute x8, starting transfers between devices, swap(): return lax.ppermute(x, AXES, [(q, q ^ mask) for q in range(device_count)])  12.7 us
    all_to_all x1, starting transfers between devices, body(): lax.all_to_all(blocks, AXES, 0, 0, axis_index_groups=groups, tiled=True)  8.36 us
    pallas_call x1, Pallas kernels, pick_rows(): pl.pallas_call(functools.partial(pick_kernel, rules, helpers), out_shape=...  2.46 us
    pallas_call x1, Pallas kernels, rebuild(): pl.pallas_call(functools.partial(finish_kernel, counts[split:], early), o...  1.06 us
  transfers between devices with their start and end apart: 9, of which 5 were waited for; matrix products, arithmetic and copies ran while one was open for 4% of the time, Pallas kernels for 1%

profile of v3, /device:TPU:0, one launch (start us, length us, event | category | flops | bytes accessed | tf_op | source)
XLA Modules:
  0.0 47.7 jit_solution(376438192424601249)
XLA Ops:
  0.0 2.5 %pick_rows.1 = (bf16[64,1024]{1,0:T(8,128)(2,1)S(1)}, bf16[128,1024]{1,0:T(8,128)(2,1)S(1)}, bf16[32,1024]{1,0:T(8,128)(2,1)S(1)}, bf16[32,1024]{1,0:T(8,128)(2,1)S(1)}, bf16[256,1024]{1,0:T(8,128)(2,1)S(1)}) custom-call(s32[22]{0:T(128)} %offset_hbm.1, s32[16,64]{1,0:T(8,128)} %bitcast.55, bf16[22,64,1024]{2,1,0:T(8,128)(2,1)} %store_ref.1), custom_call_target="tpu_custom_call" | custom-call | flops 46137344 | bytes 3932160 | tf_op jit(solution)/shard_map/pick_rows/pallas_call | solution.py:99
  2.5 0.8 %put_in_hbm.1 = bf16[256,1024]{1,0:T(8,128)(2,1)} custom-call(bf16[256,1024]{1,0:T(8,128)(2,1)S(1)} %get-tuple-element.10.rows_ref), custom_call_target="tpu_custom_call" | custom-call | bytes 1048576 | tf_op jit(solution)/shard_map/put_in_hbm/pallas_call | solution.py:136
  3.3 8.4 %all-to-all-start = ((bf16[16,16,1024]{2,1,0:T(8,128)(2,1)}), bf16[16,16,1024]{2,1,0:T(8,128)(2,1)S(1)}, u32[]{:S(2)}, u32[]{:S(2)}) async-start(bf16[16,16,1024]{2,1,0:T(8,128)(2,1)} %bitcast.38), calls=%async_computation | async-start | bytes 1048576 | tf_op jit(solution)/shard_map/all_to_all | solution.py:287
  11.7 1.8 %collective-permute-start.2 = (bf16[32,1024]{1,0:T(8,128)(2,1)S(1)}, bf16[32,1024]{1,0:T(8,128)(2,1)S(1)}, u32[]{:S(2)}, u32[]{:S(2)}) collective-permute-start(bf16[32,1024]{1,0:T(8,128)(2,1)S(1)} %get-tuple-element.13), channel_id=1, source_target_pairs={{0,20},{1,21},{2,22},{3,23},{4,16},{5,17},{6,18},{7,19},{8,28},{9,... | collective-permute-start | bytes 196616 | tf_op jit(solution)/shard_map/ppermute | solution.py:265
  13.5 3.4 %collective-permute-start.3 = (bf16[32,1024]{1,0:T(8,128)(2,1)S(1)}, bf16[32,1024]{1,0:T(8,128)(2,1)S(1)}, u32[]{:S(2)}, u32[]{:S(2)}) collective-permute-start(bf16[32,1024]{1,0:T(8,128)(2,1)S(1)} %get-tuple-element.14), channel_id=1, source_target_pairs={{0,22},{1,23},{2,20},{3,21},{4,18},{5,19},{6,16},{7,17},{8,30},{9,... | collective-permute-start | bytes 196616 | tf_op jit(solution)/shard_map/ppermute | solution.py:265
  16.9 0.5 collective-permute-start
  17.3 3.4 %collective-permute-start.1 = (bf16[128,1024]{1,0:T(8,128)(2,1)S(1)}, bf16[128,1024]{1,0:T(8,128)(2,1)S(1)}, u32[]{:S(2)}, u32[]{:S(2)}) collective-permute-start(bf16[128,1024]{1,0:T(8,128)(2,1)S(1)} %get-tuple-element.12), channel_id=1, source_target_pairs={{0,8},{1,9},{2,10},{3,11},{4,12},{5,13},{6,14},{7,15},{8,0},{9,1},... | collective-permute-start | bytes 786440 | tf_op jit(solution)/shard_map/ppermute | solution.py:265
  20.8 0.1 eq.89
  20.9 0.1 stack.131
  21.1 0.1 eq.91
  21.2 0.3 convolution_bitcast_fusion
  21.5 0.1 copy.11
  21.6 0.1 broadcast_compare_fusion
  21.7 0.3 convolution_select_fusion
  22.1 14.2 %collective-permute-done.refs_1_ = bf16[64,1024]{1,0:T(8,128)(2,1)S(1)} collective-permute-done((bf16[64,1024]{1,0:T(8,128)(2,1)S(1)}, bf16[64,1024]{1,0:T(8,128)(2,1)S(1)}, u32[]{:S(2)}, u32[]{:S(2)}) %collective-permute-start) | collective-permute-done | bytes 131104 | tf_op jit(solution)/shard_map/ppermute | solution.py:265
  36.4 0.4 fusion.10
  36.9 1.0 %collective-permute-done.4.refs_5_ = bf16[128,1024]{1,0:T(8,128)(2,1)S(1)} collective-permute-done((bf16[128,1024]{1,0:T(8,128)(2,1)S(1)}, bf16[128,1024]{1,0:T(8,128)(2,1)S(1)}, u32[]{:S(2)}, u32[]{:S(2)}) %collective-permute-start.4) | collective-permute-done | bytes 262176 | tf_op jit(solution)/shard_map/ppermute | solution.py:265
  38.0 1.5 %collective-permute-start.6 = (bf16[32,1024]{1,0:T(8,128)(2,1)S(1)}, bf16[32,1024]{1,0:T(8,128)(2,1)S(1)}, u32[]{:S(2)}, u32[]{:S(2)}) collective-permute-start(bf16[32,1024]{1,0:T(8,128)(2,1)S(1)} %pad_maximum_fusion.2), channel_id=1, source_target_pairs={{0,4},{1,5},{2,6},{3,7},{4,0},{5,1},{6,2},{7,3},{8,12},{9,13},{10,... | collective-permute-start | bytes 196616 | tf_op jit(solution)/shard_map/ppermute | solution.py:265
  39.5 1.5 %collective-permute-start.7 = (bf16[32,1024]{1,0:T(8,128)(2,1)S(1)}, bf16[32,1024]{1,0:T(8,128)(2,1)S(1)}, u32[]{:S(2)}, u32[]{:S(2)}) collective-permute-start(bf16[32,1024]{1,0:T(8,128)(2,1)S(1)} %pad_maximum_fusion.3), channel_id=1, source_target_pairs={{0,6},{1,7},{2,4},{3,5},{4,2},{5,3},{6,0},{7,1},{8,14},{9,15},{10,... | collective-permute-start | bytes 196616 | tf_op jit(solution)/shard_map/ppermute | solution.py:265
  41.0 0.6 %collective-permute-start.5 = (bf16[64,1024]{1,0:T(8,128)(2,1)S(1)}, bf16[64,1024]{1,0:T(8,128)(2,1)S(1)}, u32[]{:S(2)}, u32[]{:S(2)}) collective-permute-start(bf16[64,1024]{1,0:T(8,128)(2,1)S(1)} %pad_maximum_fusion.1), channel_id=1, source_target_pairs={{0,2},{1,3},{2,0},{3,1},{4,6},{5,7},{6,4},{7,5},{8,10},{9,11},{10,... | collective-permute-start | bytes 393224 | tf_op jit(solution)/shard_map/ppermute | solution.py:265
  41.7 0.6 %begin.1.begun_ref = f32[128,1024]{1,0:T(8,128)S(1)} custom-call(bf16[384,512]{1,0:T(8,128)(2,1)S(1)} %pad_maximum_fusion.matrix_ref, bf16[256,1024]{1,0:T(8,128)(2,1)S(1)} %bitcast.53, bf16[64,1024]{1,0:T(8,128)(2,1)S(1)} %collective-permute-done.refs_1_, bf16[128,1024]{1,0:T(8,128)(2,1)S(1)} %collective-permute-done.1.refs_2_, ...), custom_call_target="tpu_custom_call" | custom-call | flops 301989888 | bytes 1048576 | tf_op jit(solution)/shard_map/begin/pallas_call | solution.py:205
  42.3 2.9 %collective-permute-done.7.refs_2_ = bf16[32,1024]{1,0:T(8,128)(2,1)S(1)} collective-permute-done((bf16[32,1024]{1,0:T(8,128)(2,1)S(1)}, bf16[32,1024]{1,0:T(8,128)(2,1)S(1)}, u32[]{:S(2)}, u32[]{:S(2)}) %collective-permute-start.7) | collective-permute-done | bytes 65568 | tf_op jit(solution)/shard_map/ppermute | solution.py:265
  45.2 1.4 %collective-permute-done.5.refs_0_ = bf16[64,1024]{1,0:T(8,128)(2,1)S(1)} collective-permute-done((bf16[64,1024]{1,0:T(8,128)(2,1)S(1)}, bf16[64,1024]{1,0:T(8,128)(2,1)S(1)}, u32[]{:S(2)}, u32[]{:S(2)}) %collective-permute-start.5) | collective-permute-done | bytes 131104 | tf_op jit(solution)/shard_map/ppermute | solution.py:265
  46.6 1.1 %finish.1 = bf16[128,1024]{1,0:T(8,128)(2,1)} custom-call(bf16[384,512]{1,0:T(8,128)(2,1)S(1)} %pad_maximum_fusion.matrix_ref, f32[128,1024]{1,0:T(8,128)S(1)} %begin.1.begun_ref, bf16[64,1024]{1,0:T(8,128)(2,1)S(1)} %collective-permute-done.5.refs_0_, bf16[32,1024]{1,0:T(8,128)(2,1)S(1)} %collective-permute-done.6.refs_1_, ...), custom_call_target="tpu_custom_call" | custom-call | flops 100663296 | bytes 524288 | tf_op jit(solution)/shard_map/finish/pallas_call | solution.py:214
  (39 shorter events, 0.4 us)
Async XLA Ops:
  0.0 21.2 %copy-start = (f32[2,4,11]{2,1,0:T(4,128)S(1)}, f32[2,4,11]{2,1,0:T(4,128)}, u32[]{:S(2)}) copy-start(f32[2,4,11]{2,1,0:T(4,128)} %param.10) | copy-start | bytes 1060
  0.0 20.7 %copy-start.3 = (s32[22]{0:T(128)S(1)}, s32[22]{0:T(128)}, u32[]{:S(2)}) copy-start(s32[22]{0:T(128)} %offset_hbm.1) | copy-start | bytes 268
  0.0 20.7 %copy-start.1 = (s32[2,11,16]{2,0,1:T(2,128)S(1)}, s32[2,11,16]{2,0,1:T(2,128)}, u32[]{:S(2)}) copy-start(s32[2,11,16]{2,0,1:T(2,128)} %param.9) | copy-start | bytes 4228
  0.0 22.0 %copy-start.2 = (s32[2,64]{1,0:T(2,128)S(1)}, s32[2,64]{1,0:T(2,128)}, u32[]{:S(2)}) copy-start(s32[2,64]{1,0:T(2,128)} %param.11) | copy-start | bytes 1540
  3.3 38.3 %all-to-all-start = ((bf16[16,16,1024]{2,1,0:T(8,128)(2,1)}), bf16[16,16,1024]{2,1,0:T(8,128)(2,1)S(1)}, u32[]{:S(2)}, u32[]{:S(2)}) async-start(bf16[16,16,1024]{2,1,0:T(8,128)(2,1)} %bitcast.38), calls=%async_computation | async-start | bytes 1048576 | tf_op jit(solution)/shard_map/all_to_all | solution.py:287
  11.7 24.6 %collective-permute-start.2 = (bf16[32,1024]{1,0:T(8,128)(2,1)S(1)}, bf16[32,1024]{1,0:T(8,128)(2,1)S(1)}, u32[]{:S(2)}, u32[]{:S(2)}) collective-permute-start(bf16[32,1024]{1,0:T(8,128)(2,1)S(1)} %get-tuple-element.13), channel_id=1, source_target_pairs={{0,20},{1,21},{2,22},{3,23},{4,16},{5,17},{6,18},{7,19},{8,28},{9,... | collective-permute-start | bytes 196616 | tf_op jit(solution)/shard_map/ppermute | solution.py:265
  13.5 22.8 %collective-permute-start.3 = (bf16[32,1024]{1,0:T(8,128)(2,1)S(1)}, bf16[32,1024]{1,0:T(8,128)(2,1)S(1)}, u32[]{:S(2)}, u32[]{:S(2)}) collective-permute-start(bf16[32,1024]{1,0:T(8,128)(2,1)S(1)} %get-tuple-element.14), channel_id=1, source_target_pairs={{0,22},{1,23},{2,20},{3,21},{4,18},{5,19},{6,16},{7,17},{8,30},{9,... | collective-permute-start | bytes 196616 | tf_op jit(solution)/shard_map/ppermute | solution.py:265
  16.9 19.4 %collective-permute-start = (bf16[64,1024]{1,0:T(8,128)(2,1)S(1)}, bf16[64,1024]{1,0:T(8,128)(2,1)S(1)}, u32[]{:S(2)}, u32[]{:S(2)}) collective-permute-start(bf16[64,1024]{1,0:T(8,128)(2,1)S(1)} %get-tuple-element.11), channel_id=1, source_target_pairs={{0,16},{1,17},{2,18},{3,19},{4,20},{5,21},{6,22},{7,23},{8,24},{9,... | collective-permute-start | bytes 393224 | tf_op jit(solution)/shard_map/ppermute | solution.py:265
  17.3 18.9 %collective-permute-start.1 = (bf16[128,1024]{1,0:T(8,128)(2,1)S(1)}, bf16[128,1024]{1,0:T(8,128)(2,1)S(1)}, u32[]{:S(2)}, u32[]{:S(2)}) collective-permute-start(bf16[128,1024]{1,0:T(8,128)(2,1)S(1)} %get-tuple-element.12), channel_id=1, source_target_pairs={{0,8},{1,9},{2,10},{3,11},{4,12},{5,13},{6,14},{7,15},{8,0},{9,1},... | collective-permute-start | bytes 786440 | tf_op jit(solution)/shard_map/ppermute | solution.py:265
  36.4 1.6 %collective-permute-start.4 = (bf16[128,1024]{1,0:T(8,128)(2,1)S(1)}, bf16[128,1024]{1,0:T(8,128)(2,1)S(1)}, u32[]{:S(2)}, u32[]{:S(2)}) collective-permute-start(bf16[128,1024]{1,0:T(8,128)(2,1)S(1)} %get-tuple-element.18), channel_id=1, source_target_pairs={{0,1},{1,0},{2,3},{3,2},{4,5},{5,4},{6,7},{7,6},{8,9},{9,8},{10,11... | collective-permute-start | bytes 786440 | tf_op jit(solution)/shard_map/ppermute | solution.py:265
  38.0 4.3 %collective-permute-start.6 = (bf16[32,1024]{1,0:T(8,128)(2,1)S(1)}, bf16[32,1024]{1,0:T(8,128)(2,1)S(1)}, u32[]{:S(2)}, u32[]{:S(2)}) collective-permute-start(bf16[32,1024]{1,0:T(8,128)(2,1)S(1)} %pad_maximum_fusion.2), channel_id=1, source_target_pairs={{0,4},{1,5},{2,6},{3,7},{4,0},{5,1},{6,2},{7,3},{8,12},{9,13},{10,... | collective-permute-start | bytes 196616 | tf_op jit(solution)/shard_map/ppermute | solution.py:265
  39.5 5.7 %collective-permute-start.7 = (bf16[32,1024]{1,0:T(8,128)(2,1)S(1)}, bf16[32,1024]{1,0:T(8,128)(2,1)S(1)}, u32[]{:S(2)}, u32[]{:S(2)}) collective-permute-start(bf16[32,1024]{1,0:T(8,128)(2,1)S(1)} %pad_maximum_fusion.3), channel_id=1, source_target_pairs={{0,6},{1,7},{2,4},{3,5},{4,2},{5,3},{6,0},{7,1},{8,14},{9,15},{10,... | collective-permute-start | bytes 196616 | tf_op jit(solution)/shard_map/ppermute | solution.py:265
  41.0 5.6 %collective-permute-start.5 = (bf16[64,1024]{1,0:T(8,128)(2,1)S(1)}, bf16[64,1024]{1,0:T(8,128)(2,1)S(1)}, u32[]{:S(2)}, u32[]{:S(2)}) collective-permute-start(bf16[64,1024]{1,0:T(8,128)(2,1)S(1)} %pad_maximum_fusion.1), channel_id=1, source_target_pairs={{0,2},{1,3},{2,0},{3,1},{4,6},{5,7},{6,4},{7,5},{8,10},{9,11},{10,... | collective-permute-start | bytes 393224 | tf_op jit(solution)/shard_map/ppermute | solution.py:265
